TPU v7x, 128 devices: a whole 4x4x4 slice. The times are simulated.
128 devices in a mesh: usr: 16 (over z_hi, y, core), itm: 8 (over x, z_lo).
Axes of the slice: x: 4, y: 4, z: 4 (z_hi: 2, z_lo: 2; z = z_hi * 2 + z_lo), core: 2. Of those that a mesh axis runs over, the one named last changes fastest.
Arguments:
- ratings: bfloat16 [16384, 16384], P('usr', 'itm'), may hold values from -6 to 6
- tile_mask: int32 [128, 128], P('usr', 'itm'), may hold values 0 or 1
- counts: int32 [16], P('usr'), may hold values from 256 to 1024
- users: float32 [16384, 256], P(('usr', 'itm')), may hold values from -1.5 to 1.5
- items: float32 [16384, 256], P(('itm', 'usr')), may hold values from -1.5 to 1.5
- user_mom: float32 [16384, 256], P(('usr', 'itm')), may hold values from -6 to 6
- item_mom: float32 [16384, 256], P(('itm', 'usr')), may hold values from -6 to 6
- user_accept: int32 [128], P(('usr', 'itm')), may hold values 0 or 1
- item_accept: int32 [128], P(('itm', 'usr')), may hold values 0 or 1
Outputs:
- users_out: float32 [16384, 256], P(('usr', 'itm'))
- items_out: float32 [16384, 256], P(('itm', 'usr'))
- user_mom_out: float32 [16384, 256], P(('usr', 'itm'))
- item_mom_out: float32 [16384, 256], P(('itm', 'usr'))
All inputs are finite; a program needn't handle non-finite values. No bound on the sum of `tile_mask` or of `user_accept` or of `item_accept` on one device may be relied on, other than what follows from the above.
Results may differ from a plain program's by a relative error of at most 0.01.
Values may be sent and summed in bfloat16 or wider, within the bound.
No kernel may reach another device: no remote copies, remote signals or barrier semaphores. Data moves between devices by JAX's collectives and lax.ppermute only.
A program may use at most 64 MiB of HBM per device.

v0:
```python
import jax
import jax.numpy as jnp
from jax import lax
from jax.sharding import PartitionSpec as P

BLK = 128
LEAPS = 2


step_size = 0.02


def in_order(tiles, dim):
    dims = list(tiles.shape[1:])
    dims[dim] *= tiles.shape[0]
    return jnp.moveaxis(tiles, 0, dim).reshape(dims)


def from_everyone(array, axis):
    size = lax.axis_size(axis)
    return lax.all_to_all(
        jnp.broadcast_to(array[None], (size, *array.shape)), axis, 0, 0, tiled=True
    )


def gathered_copies(array, axis, dim):
    return in_order(from_everyone(array, axis), dim)


def split_up(array, dim, size):
    before, after = (array.shape[:dim], array.shape[dim + 1 :])
    return jnp.moveaxis(array.reshape(*before, size, -1, *after), dim, 0)


def summed_on_arrival(array, axis, dim):
    tiles = split_up(array, dim, lax.axis_size(axis))
    arrived = lax.all_to_all(tiles, axis, split_axis=0, concat_axis=0, tiled=True)
    return arrived.astype(jnp.float32).sum(axis=0)


def body(ratings, tile_mask, counts, users, items, user_mom, item_mom, user_accept, item_accept):
    group_rows = ratings.shape[0]
    colmask = jnp.repeat(tile_mask, BLK, axis=1).astype(jnp.float32)
    alive = (jnp.arange(group_rows, dtype=jnp.int32) < counts[0]).astype(jnp.float32)

    def gradients(user_pos, item_pos):
        full_users = gathered_copies(user_pos.astype(jnp.bfloat16), "itm", 0)
        piece = gathered_copies(item_pos.astype(jnp.bfloat16), "usr", 0)
        count = piece.shape[0]
        guess = jnp.dot(full_users, piece.T, preferred_element_type=jnp.float32)
        error = (ratings.astype(jnp.float32) - guess).reshape(
            group_rows // BLK, BLK, count
        ) * colmask[:, None, :]
        error = (error.reshape(group_rows, count) * alive[:, None]).astype(jnp.bfloat16)
        user_sum = jnp.dot(error, piece, preferred_element_type=jnp.float32)
        item_part = jnp.dot(error.T, full_users, preferred_element_type=jnp.float32)
        item_sum = item_part
        user_sum, item_sum = (user_sum, item_sum)
        user_part = summed_on_arrival(user_sum.astype(jnp.bfloat16), "itm", 0)
        item_part = summed_on_arrival(item_sum.astype(jnp.bfloat16), "usr", 0)
        return (user_pos - user_part, item_pos - item_part)

    user_pos, item_pos = (users, items)
    user_grad, item_grad = gradients(user_pos, item_pos)
    for leap in range(LEAPS):
        user_mom = user_mom - 0.5 * step_size * user_grad
        item_mom = item_mom - 0.5 * step_size * item_grad
        user_pos = user_pos + step_size * user_mom
        item_pos = item_pos + step_size * item_mom
        user_grad, item_grad = gradients(user_pos, item_pos)
        user_mom = user_mom - 0.5 * step_size * user_grad
        item_mom = item_mom - 0.5 * step_size * item_grad
    user_take = jnp.repeat(user_accept, BLK)[:, None] > 0
    item_take = jnp.repeat(item_accept, BLK)[:, None] > 0
    return (
        jnp.where(user_take, user_pos, users),
        jnp.where(item_take, item_pos, items),
        user_mom,
        item_mom,
    )


def solution(mesh):
    in_specs = (
        P("usr", "itm"),
        P("usr", "itm"),
        P("usr"),
        P(("usr", "itm"), None),
        P(("itm", "usr"), None),
        P(("usr", "itm"), None),
        P(("itm", "usr"), None),
        P(("usr", "itm")),
        P(("itm", "usr")),
    )
    out_specs = (
        P(("usr", "itm"), None),
        P(("itm", "usr"), None),
        P(("usr", "itm"), None),
        P(("itm", "usr"), None),
    )
    return jax.shard_map(body, mesh=mesh, in_specs=in_specs, out_specs=out_specs, check_vma=False)
```

profile of v0, /device:TPU:0, one launch (start us, length us, event | category | flops | bytes accessed | tf_op | source)
XLA Modules:
  0.0 235.9 jit_solution(3670549589512572605)
XLA Ops:
  2.4 5.7 %all-to-all-start = ((bf16[8,128,256]{2,1,0:T(8,128)(2,1)}), bf16[8,128,256]{2,1,0:T(8,128)(2,1)S(1)}, u32[]{:S(2)}, u32[]{:S(2)}) async-start(bf16[8,128,256]{2,1,0:T(8,128)(2,1)} %broadcast_in_dim.25), calls=%async_computation | async-start | bytes 1048576 | tf_op jit(solution)/shard_map/all_to_all | solution.py:21
  9.0 8.6 %all-to-all-done = bf16[8,128,256]{2,1,0:T(8,128)(2,1)S(1)} async-done(((bf16[8,128,256]{2,1,0:T(8,128)(2,1)}), bf16[8,128,256]{2,1,0:T(8,128)(2,1)S(1)}, u32[]{:S(2)}, u32[]{:S(2)}) %all-to-all-start) | async-done | bytes 524320 | tf_op jit(solution)/shard_map/all_to_all | solution.py:21
  18.7 7.6 %all-to-all-start.1 = ((bf16[16,128,256]{2,1,0:T(8,128)(2,1)}), bf16[16,128,256]{2,1,0:T(8,128)(2,1)S(1)}, u32[]{:S(2)}, u32[]{:S(2)}) async-start(bf16[16,128,256]{2,1,0:T(8,128)(2,1)} %broadcast_in_dim.26), calls=%async_computation.1 | async-start | bytes 2097152 | tf_op jit(solution)/shard_map/all_to_all | solution.py:21
  27.1 17.2 %all-to-all-done.1 = bf16[16,128,256]{2,1,0:T(8,128)(2,1)S(1)} async-done(((bf16[16,128,256]{2,1,0:T(8,128)(2,1)}), bf16[16,128,256]{2,1,0:T(8,128)(2,1)S(1)}, u32[]{:S(2)}, u32[]{:S(2)}) %all-to-all-start.1) | async-done | bytes 1048608 | tf_op jit(solution)/shard_map/all_to_all | solution.py:21
  44.3 3.6 %fusion.1 = bf16[1024,2048]{1,0:T(8,128)(2,1)S(1)} fusion(bf16[1024,2048]{1,0:T(8,128)(2,1)} %param.9, bf16[1024,256]{1,0:T(8,128)(2,1)S(1)} %bitcast.58, bf16[2048,256]{1,0:T(8,128)(2,1)S(1)} %bitcast.52, f32[1024]{0:T(1024)S(1)} %fusion.8, f32[8,2048]{1,0:T(8,128)S(1)} %broadcast_bitcast_fusion), kind=kOutput, calls=%fused_computation.7 | convolution fusion | flops 1084227584 | bytes 10031104 | tf_op jit(solution)/shard_map/dot_general | solution.py:50
  50.0 3.5 %all-to-all-start.2 = ((bf16[8,128,256]{2,1,0:T(8,128)(2,1)}), bf16[8,128,256]{2,1,0:T(8,128)(2,1)S(1)}, u32[]{:S(2)}, u32[]{:S(2)}) async-start(bf16[8,128,256]{2,1,0:T(8,128)(2,1)} %bitcast.6), calls=%async_computation.2 | async-start | bytes 1048576 | tf_op jit(solution)/shard_map/all_to_all | solution.py:37
  53.6 4.6 %convolution_convert_fusion.2 = bf16[2048,256]{1,0:T(8,128)(2,1)} fusion(bf16[1024,2048]{1,0:T(8,128)(2,1)} %copy-done.1, bf16[1024,256]{1,0:T(8,128)(2,1)S(1)} %bitcast.59), kind=kOutput, calls=%fused_computation.14 | convolution fusion | flops 1074266112 | bytes 5767168 | tf_op jit(solution)/shard_map/dot_general | solution.py:56
  58.1 5.0 %all-to-all-done.2 = bf16[8,128,256]{2,1,0:T(8,128)(2,1)S(1)} async-done(((bf16[8,128,256]{2,1,0:T(8,128)(2,1)}), bf16[8,128,256]{2,1,0:T(8,128)(2,1)S(1)}, u32[]{:S(2)}, u32[]{:S(2)}) %all-to-all-start.2) | async-done | bytes 524320 | tf_op jit(solution)/shard_map/all_to_all | solution.py:37
  63.2 3.7 %all-to-all-start.4 = ((bf16[16,128,256]{2,1,0:T(8,128)(2,1)}), bf16[16,128,256]{2,1,0:T(8,128)(2,1)S(1)}, u32[]{:S(2)}, u32[]{:S(2)}) async-start(bf16[16,128,256]{2,1,0:T(8,128)(2,1)} %bitcast.66), calls=%async_computation.4 | async-start | bytes 2097152 | tf_op jit(solution)/shard_map/all_to_all | solution.py:37
  67.0 17.8 %all-to-all-done.4 = bf16[16,128,256]{2,1,0:T(8,128)(2,1)S(1)} async-done(((bf16[16,128,256]{2,1,0:T(8,128)(2,1)}), bf16[16,128,256]{2,1,0:T(8,128)(2,1)S(1)}, u32[]{:S(2)}, u32[]{:S(2)}) %all-to-all-start.4) | async-done | bytes 1048608 | tf_op jit(solution)/shard_map/all_to_all | solution.py:37
  89.3 9.4 %all-to-all-done.3 = bf16[8,128,256]{2,1,0:T(8,128)(2,1)S(1)} async-done(((bf16[8,128,256]{2,1,0:T(8,128)(2,1)}), bf16[8,128,256]{2,1,0:T(8,128)(2,1)S(1)}, u32[]{:S(2)}, u32[]{:S(2)}) %all-to-all-start.3) | async-done | bytes 524320 | tf_op jit(solution)/shard_map/all_to_all | solution.py:21
  98.8 20.9 %all_to_all.60 = bf16[16,128,256]{2,1,0:T(8,128)(2,1)S(1)} all-to-all(bf16[16,128,256]{2,1,0:T(8,128)(2,1)S(1)} %broadcast_in_dim.29), channel_id=1, replica_groups=mesh['usr'=16,'itm'=8] {'usr'}, dimensions={0} | all-to-all | bytes 2097152 | tf_op jit(solution)/shard_map/all_to_all | solution.py:21
  119.7 3.6 %fusion.3 = bf16[1024,2048]{1,0:T(8,128)(2,1)S(1)} fusion(bf16[1024,2048]{1,0:T(8,128)(2,1)} %param.9, bf16[1024,256]{1,0:T(8,128)(2,1)S(1)} %bitcast.62, bf16[2048,256]{1,0:T(8,128)(2,1)S(1)} %bitcast.56, f32[1024]{0:T(1024)S(1)} %fusion.8, f32[8,2048]{1,0:T(8,128)S(1)} %broadcast_bitcast_fusion), kind=kOutput, calls=%fused_computation.9 | convolution fusion | flops 1084227584 | bytes 10031104 | tf_op jit(solution)/shard_map/dot_general | solution.py:50
  129.0 4.5 %convolution_convert_fusion.1 = bf16[2048,256]{1,0:T(8,128)(2,1)} fusion(bf16[1024,2048]{1,0:T(8,128)(2,1)} %copy-done.2, bf16[1024,256]{1,0:T(8,128)(2,1)S(1)} %bitcast.63), kind=kOutput, calls=%fused_computation.13 | convolution fusion | flops 1074266112 | bytes 5767168 | tf_op jit(solution)/shard_map/dot_general | solution.py:56
  133.5 4.8 %all-to-all-done.6 = bf16[8,128,256]{2,1,0:T(8,128)(2,1)S(1)} async-done(((bf16[8,128,256]{2,1,0:T(8,128)(2,1)}), bf16[8,128,256]{2,1,0:T(8,128)(2,1)S(1)}, u32[]{:S(2)}, u32[]{:S(2)}) %all-to-all-start.6) | async-done | bytes 524320 | tf_op jit(solution)/shard_map/all_to_all | solution.py:37
  138.3 3.7 %all-to-all-start.7 = ((bf16[16,128,256]{2,1,0:T(8,128)(2,1)}), bf16[16,128,256]{2,1,0:T(8,128)(2,1)S(1)}, u32[]{:S(2)}, u32[]{:S(2)}) async-start(bf16[16,128,256]{2,1,0:T(8,128)(2,1)} %bitcast.65), calls=%async_computation.7 | async-start | bytes 2097152 | tf_op jit(solution)/shard_map/all_to_all | solution.py:37
  142.1 17.8 %all-to-all-done.7 = bf16[16,128,256]{2,1,0:T(8,128)(2,1)S(1)} async-done(((bf16[16,128,256]{2,1,0:T(8,128)(2,1)}), bf16[16,128,256]{2,1,0:T(8,128)(2,1)S(1)}, u32[]{:S(2)}, u32[]{:S(2)}) %all-to-all-start.7) | async-done | bytes 1048608 | tf_op jit(solution)/shard_map/all_to_all | solution.py:37
  164.5 9.4 %all-to-all-done.8 = bf16[8,128,256]{2,1,0:T(8,128)(2,1)S(1)} async-done(((bf16[8,128,256]{2,1,0:T(8,128)(2,1)}), bf16[8,128,256]{2,1,0:T(8,128)(2,1)S(1)}, u32[]{:S(2)}, u32[]{:S(2)}) %all-to-all-start.8) | async-done | bytes 524320 | tf_op jit(solution)/shard_map/all_to_all | solution.py:21
  174.0 20.9 %all_to_all.61 = bf16[16,128,256]{2,1,0:T(8,128)(2,1)S(1)} all-to-all(bf16[16,128,256]{2,1,0:T(8,128)(2,1)S(1)} %broadcast_in_dim.32), channel_id=1, replica_groups=mesh['usr'=16,'itm'=8] {'usr'}, dimensions={0} | all-to-all | bytes 2097152 | tf_op jit(solution)/shard_map/all_to_all | solution.py:21
  194.9 3.6 %fusion.5 = bf16[1024,2048]{1,0:T(8,128)(2,1)S(1)} fusion(bf16[1024,2048]{1,0:T(8,128)(2,1)} %param.9, bf16[1024,256]{1,0:T(8,128)(2,1)S(1)} %bitcast.60, bf16[2048,256]{1,0:T(8,128)(2,1)S(1)} %bitcast.54, f32[1024]{0:T(1024)S(1)} %fusion.8, f32[8,2048]{1,0:T(8,128)S(1)} %broadcast_bitcast_fusion), kind=kOutput, calls=%fused_computation.11 | convolution fusion | flops 1084227584 | bytes 10031104 | tf_op jit(solution)/shard_map/dot_general | solution.py:50
  204.2 4.5 %convolution_convert_fusion = bf16[2048,256]{1,0:T(8,128)(2,1)} fusion(bf16[1024,2048]{1,0:T(8,128)(2,1)} %copy-done, bf16[1024,256]{1,0:T(8,128)(2,1)S(1)} %bitcast.61), kind=kOutput, calls=%fused_computation.12 | convolution fusion | flops 1074266112 | bytes 5767168 | tf_op jit(solution)/shard_map/dot_general | solution.py:56
  208.7 4.8 %all-to-all-done.10 = bf16[8,128,256]{2,1,0:T(8,128)(2,1)S(1)} async-done(((bf16[8,128,256]{2,1,0:T(8,128)(2,1)}), bf16[8,128,256]{2,1,0:T(8,128)(2,1)S(1)}, u32[]{:S(2)}, u32[]{:S(2)}) %all-to-all-start.10) | async-done | bytes 524320 | tf_op jit(solution)/shard_map/all_to_all | solution.py:37
  213.5 3.7 %all-to-all-start.11 = ((bf16[16,128,256]{2,1,0:T(8,128)(2,1)}), bf16[16,128,256]{2,1,0:T(8,128)(2,1)S(1)}, u32[]{:S(2)}, u32[]{:S(2)}) async-start(bf16[16,128,256]{2,1,0:T(8,128)(2,1)} %bitcast.64), calls=%async_computation.11 | async-start | bytes 2097152 | tf_op jit(solution)/shard_map/all_to_all | solution.py:37
  219.2 15.8 %all-to-all-done.11 = bf16[16,128,256]{2,1,0:T(8,128)(2,1)S(1)} async-done(((bf16[16,128,256]{2,1,0:T(8,128)(2,1)}), bf16[16,128,256]{2,1,0:T(8,128)(2,1)S(1)}, u32[]{:S(2)}, u32[]{:S(2)}) %all-to-all-start.11) | async-done | bytes 1048608 | tf_op jit(solution)/shard_map/all_to_all | solution.py:37
  (47 shorter events, 28.4 us)
Async XLA Ops:
  0.6 26.3 %copy-start.7 = (s32[8,16]{1,0:T(8,128)S(1)}, s32[8,16]{1,0:T(8,128)}, u32[]{:S(2)}) copy-start(s32[8,16]{1,0:T(8,128)} %param.10) | copy-start | bytes 1540
  2.4 15.2 %all-to-all-start = ((bf16[8,128,256]{2,1,0:T(8,128)(2,1)}), bf16[8,128,256]{2,1,0:T(8,128)(2,1)S(1)}, u32[]{:S(2)}, u32[]{:S(2)}) async-start(bf16[8,128,256]{2,1,0:T(8,128)(2,1)} %broadcast_in_dim.25), calls=%async_computation | async-start | bytes 1048576 | tf_op jit(solution)/shard_map/all_to_all | solution.py:21
  18.7 25.6 %all-to-all-start.1 = ((bf16[16,128,256]{2,1,0:T(8,128)(2,1)}), bf16[16,128,256]{2,1,0:T(8,128)(2,1)S(1)}, u32[]{:S(2)}, u32[]{:S(2)}) async-start(bf16[16,128,256]{2,1,0:T(8,128)(2,1)} %broadcast_in_dim.26), calls=%async_computation.1 | async-start | bytes 2097152 | tf_op jit(solution)/shard_map/all_to_all | solution.py:21
  47.9 2.1 copy-start.1
  50.0 13.1 %all-to-all-start.2 = ((bf16[8,128,256]{2,1,0:T(8,128)(2,1)}), bf16[8,128,256]{2,1,0:T(8,128)(2,1)S(1)}, u32[]{:S(2)}, u32[]{:S(2)}) async-start(bf16[8,128,256]{2,1,0:T(8,128)(2,1)} %bitcast.6), calls=%async_computation.2 | async-start | bytes 1048576 | tf_op jit(solution)/shard_map/all_to_all | solution.py:37
  53.5 13.4 %copy-start.3 = (f32[128,256]{1,0:T(8,128)S(1)}, f32[128,256]{1,0:T(8,128)}, u32[]{:S(2)}) copy-start(f32[128,256]{1,0:T(8,128)} %param.12) | copy-start | bytes 393220
  53.6 13.4 %copy-start.5 = (f32[128,256]{1,0:T(8,128)S(1)}, f32[128,256]{1,0:T(8,128)}, u32[]{:S(2)}) copy-start(f32[128,256]{1,0:T(8,128)} %param.14) | copy-start | bytes 393220
  58.1 31.1 %copy-start.4 = (f32[128,256]{1,0:T(8,128)S(1)}, f32[128,256]{1,0:T(8,128)}, u32[]{:S(2)}) copy-start(f32[128,256]{1,0:T(8,128)} %param.13) | copy-start | bytes 393220
  58.1 31.1 %copy-start.6 = (f32[128,256]{1,0:T(8,128)S(1)}, f32[128,256]{1,0:T(8,128)}, u32[]{:S(2)}) copy-start(f32[128,256]{1,0:T(8,128)} %param.15) | copy-start | bytes 393220
  63.2 21.6 %all-to-all-start.4 = ((bf16[16,128,256]{2,1,0:T(8,128)(2,1)}), bf16[16,128,256]{2,1,0:T(8,128)(2,1)S(1)}, u32[]{:S(2)}, u32[]{:S(2)}) async-start(bf16[16,128,256]{2,1,0:T(8,128)(2,1)} %bitcast.66), calls=%async_computation.4 | async-start | bytes 2097152 | tf_op jit(solution)/shard_map/all_to_all | solution.py:37
  85.6 13.1 %all-to-all-start.3 = ((bf16[8,128,256]{2,1,0:T(8,128)(2,1)}), bf16[8,128,256]{2,1,0:T(8,128)(2,1)S(1)}, u32[]{:S(2)}, u32[]{:S(2)}) async-start(bf16[8,128,256]{2,1,0:T(8,128)(2,1)} %broadcast_in_dim.28), calls=%async_computation.3 | async-start | bytes 1048576 | tf_op jit(solution)/shard_map/all_to_all | solution.py:21
  123.4 2.1 copy-start.2
  125.5 12.8 %all-to-all-start.6 = ((bf16[8,128,256]{2,1,0:T(8,128)(2,1)}), bf16[8,128,256]{2,1,0:T(8,128)(2,1)S(1)}, u32[]{:S(2)}, u32[]{:S(2)}) async-start(bf16[8,128,256]{2,1,0:T(8,128)(2,1)} %bitcast.10), calls=%async_computation.6 | async-start | bytes 1048576 | tf_op jit(solution)/shard_map/all_to_all | solution.py:37
  138.3 21.6 %all-to-all-start.7 = ((bf16[16,128,256]{2,1,0:T(8,128)(2,1)}), bf16[16,128,256]{2,1,0:T(8,128)(2,1)S(1)}, u32[]{:S(2)}, u32[]{:S(2)}) async-start(bf16[16,128,256]{2,1,0:T(8,128)(2,1)} %bitcast.65), calls=%async_computation.7 | async-start | bytes 2097152 | tf_op jit(solution)/shard_map/all_to_all | solution.py:37
  160.7 13.1 %all-to-all-start.8 = ((bf16[8,128,256]{2,1,0:T(8,128)(2,1)}), bf16[8,128,256]{2,1,0:T(8,128)(2,1)S(1)}, u32[]{:S(2)}, u32[]{:S(2)}) async-start(bf16[8,128,256]{2,1,0:T(8,128)(2,1)} %broadcast_in_dim.31), calls=%async_computation.8 | async-start | bytes 1048576 | tf_op jit(solution)/shard_map/all_to_all | solution.py:21
  198.5 2.1 copy-start
  200.7 12.8 %all-to-all-start.10 = ((bf16[8,128,256]{2,1,0:T(8,128)(2,1)}), bf16[8,128,256]{2,1,0:T(8,128)(2,1)S(1)}, u32[]{:S(2)}, u32[]{:S(2)}) async-start(bf16[8,128,256]{2,1,0:T(8,128)(2,1)} %bitcast.15), calls=%async_computation.10 | async-start | bytes 1048576 | tf_op jit(solution)/shard_map/all_to_all | solution.py:37
  213.5 21.6 %all-to-all-start.11 = ((bf16[16,128,256]{2,1,0:T(8,128)(2,1)}), bf16[16,128,256]{2,1,0:T(8,128)(2,1)S(1)}, u32[]{:S(2)}, u32[]{:S(2)}) async-start(bf16[16,128,256]{2,1,0:T(8,128)(2,1)} %bitcast.64), calls=%async_computation.11 | async-start | bytes 2097152 | tf_op jit(solution)/shard_map/all_to_all | solution.py:37
where the time goes:
time: 238 us; the launch traced here: 236 us
  waiting for transfers between devices  111 us (47%)
  blocking collectives  41.8 us (18%)
  starting transfers between devices  41.7 us (18%)
  matrix products  30.9 us (13%)
  other arithmetic  4.13 us (2%)
  local copies, waits for them, and re-layouts  3.93 us (2%)
  between operations  2.86 us (1%)
    all_to_all x6, waiting for transfers between devices, summed_on_arrival(): lax.all_to_all(tiles, axis, split_axis=0, concat_axis=0, tiled=True)  66 us
    all_to_all x4, waiting for transfers between devices, from_everyone(): lax.all_to_all(jnp.broadcast_to(array[None], (size, *array.shape)), axis,...  44.6 us
    all_to_all x2, blocking collectives, from_everyone(): lax.all_to_all(jnp.broadcast_to(array[None], (size, *array.shape)), axis,...  41.8 us
    all_to_all x6, starting transfers between devices, summed_on_arrival(): lax.all_to_all(tiles, axis, split_axis=0, concat_axis=0, tiled=True)  21.4 us
    all_to_all x4, starting transfers between devices, from_everyone(): lax.all_to_all(jnp.broadcast_to(array[None], (size, *array.shape)), axis,...  20.3 us
    dot_general x3, matrix products, gradients(): item_part = jnp.dot(error.T, full_users, preferred_element_type=jnp.float32)  13.6 us
    dot_general x3, matrix products, gradients(): guess = jnp.dot(full_users, piece.T, preferred_element_type=jnp.float32)  10.9 us
    dot_general x3, matrix products, gradients(): user_sum = jnp.dot(error, piece, preferred_element_type=jnp.float32)  6.39 us
  transfers between devices with their start and end apart: 10, of which 10 were waited for; matrix products, arithmetic and copies ran while one was open for 7% of the time, Pallas kernels for 0%

commit v1 on v0

v1 whole, which is shorter than its diff:
```python
import jax
import jax.numpy as jnp
from jax import lax
from jax.sharding import PartitionSpec as P

BLK = 128
LEAPS = 2
step_size = 0.02
BF = jnp.bfloat16
F32 = jnp.float32


def swap(array, axis, bits):
    size = lax.axis_size(axis)
    return lax.ppermute(array, axis, [(i, i ^ bits) for i in range(size)])


def pick(array, index):
    return lax.dynamic_index_in_dim(array, index, 0, keepdims=False)


def absolute(pieces, index):
    stack = jnp.stack(pieces)
    return jnp.stack([pick(stack, index ^ k) for k in range(len(pieces))])


def body(ratings, tile_mask, counts, users, items, user_mom, item_mom, user_accept, item_accept):
    rows, cols = ratings.shape
    K = users.shape[1]
    u = lax.axis_index("usr")
    i = lax.axis_index("itm")
    zh, y, c = u // 8, (u // 2) % 4, u % 2
    x, zl = i // 2, i % 2
    colmask = jnp.repeat(tile_mask, BLK, axis=1).astype(F32)
    alive = (jnp.arange(rows, dtype=jnp.int32) < counts[0]).astype(F32)

    def compute(full_users, piece):
        guess = jnp.dot(full_users, piece.T, preferred_element_type=F32)
        error = (ratings.astype(F32) - guess).reshape(rows // BLK, BLK, cols) * colmask[:, None, :]
        error = (error.reshape(rows, cols) * alive[:, None]).astype(BF)
        user_sum = jnp.dot(error, piece, preferred_element_type=F32)
        item_sum = jnp.dot(error.T, full_users, preferred_element_type=F32)
        return user_sum.astype(BF), item_sum.astype(BF)

    def gather_users(pair):
        pieces = [pair] + [swap(pair, "itm", 2 * k) for k in (1, 2, 3)]
        return absolute(pieces, x).reshape(rows, K)

    def gather_items(pair):
        pieces = [pair] + [swap(pair, "usr", 2 * k) for k in (1, 2, 3)]
        half = absolute(pieces, y)
        other = swap(half, "usr", 1)
        both = absolute([half, other], c)
        return both.transpose(2, 1, 0, 3, 4).reshape(cols, K)

    def reduce_users(part):
        part = part.reshape(4, 2, BLK, K)
        got = [swap(pick(part, x ^ k), "itm", 2 * k).astype(F32) for k in (1, 2, 3)]
        return (pick(part, x).astype(F32) + got[0] + got[1] + got[2]).astype(BF)

    def reduce_items(part):
        part = part.reshape(2, 4, 2, BLK, K).transpose(2, 1, 0, 3, 4)
        half = pick(part, c).astype(F32) + swap(pick(part, 1 - c), "usr", 1).astype(F32)
        half = half.astype(BF)
        got = [swap(pick(half, y ^ k), "usr", 2 * k).astype(F32) for k in (1, 2, 3)]
        return (pick(half, y).astype(F32) + got[0] + got[1] + got[2]).astype(BF)

    def pair_of(mine, other, z):
        return absolute([mine, other], z)

    def split(pos):
        high = pos.astype(BF)
        return high, (pos - high.astype(F32)).astype(BF)

    uh, ul = split(users)
    vh, vl = split(items)
    uh_o, vh_o = swap(uh, "itm", 1), swap(vh, "usr", 8)
    ul_o, vl_o = swap(jnp.stack([ul, user_mom.astype(BF)]), "itm", 1), swap(jnp.stack([vl, item_mom.astype(BF)]), "usr", 8)
    user_bf, item_bf = pair_of(uh, uh_o, zl), pair_of(vh, vh_o, zh)
    up = pair_of(users, uh_o.astype(F32) + ul_o[0].astype(F32), zl)
    vp = pair_of(items, vh_o.astype(F32) + vl_o[0].astype(F32), zh)
    um = pair_of(user_mom, ul_o[1].astype(F32), zl)
    vm = pair_of(item_mom, vl_o[1].astype(F32), zh)

    half_step = 0.5 * step_size
    for leap in range(LEAPS):
        gu, gv = compute(gather_users(user_bf), gather_items(item_bf))
        su, sv = reduce_users(gu), reduce_items(gv)
        eu = su.astype(F32) + swap(su, "itm", 1).astype(F32)
        ev = sv.astype(F32) + swap(sv, "usr", 8).astype(F32)
        scale = half_step if leap == 0 else 2 * half_step
        um = um - scale * (up - eu)
        vm = vm - scale * (vp - ev)
        up = up + step_size * um
        vp = vp + step_size * vm
        user_bf, item_bf = up.astype(BF), vp.astype(BF)
    gu, gv = compute(gather_users(user_bf), gather_items(item_bf))
    su, sv = reduce_users(gu), reduce_items(gv)
    eu = pick(su, zl).astype(F32) + swap(pick(su, 1 - zl), "itm", 1).astype(F32)
    ev = pick(sv, zh).astype(F32) + swap(pick(sv, 1 - zh), "usr", 8).astype(F32)
    up, vp, um, vm = pick(up, zl), pick(vp, zh), pick(um, zl), pick(vm, zh)
    um = um - half_step * (up - eu)
    vm = vm - half_step * (vp - ev)
    user_take = jnp.repeat(user_accept, BLK)[:, None] > 0
    item_take = jnp.repeat(item_accept, BLK)[:, None] > 0
    return (
        jnp.where(user_take, up, users),
        jnp.where(item_take, vp, items),
        um,
        vm,
    )


def solution(mesh):
    in_specs = (
        P("usr", "itm"),
        P("usr", "itm"),
        P("usr"),
        P(("usr", "itm"), None),
        P(("itm", "usr"), None),
        P(("usr", "itm"), None),
        P(("itm", "usr"), None),
        P(("usr", "itm")),
        P(("itm", "usr")),
    )
    out_specs = (
        P(("usr", "itm"), None),
        P(("itm", "usr"), None),
        P(("usr", "itm"), None),
        P(("itm", "usr"), None),
    )
    return jax.shard_map(body, mesh=mesh, in_specs=in_specs, out_specs=out_specs, check_vma=False)
```

time: 238 us -> 149 us (0.63)
  waiting for transfers between devices: 111 us -> 54.2 us
  blocking collectives: 41.8 us -> 0 us
  starting transfers between devices: 41.7 us -> 65.5 us
  matrix products: 30.9 us -> 12.6 us
  other arithmetic: 4.13 us -> 10.2 us
    all_to_all x10 -> x0, waiting for transfers between devices: 111 us -> none  [the longest x6 66 us: summed_on_arrival(): lax.all_to_all(tiles, axis, split_axis=0, concat_axis=0, tiled=True)]
    ppermute x0 -> x52, starting transfers between devices: none -> 65.5 us  [swap(): return lax.ppermute(array, axis, [(i, i ^ bits) for i in range(size)])]
    ppermute x0 -> x52, waiting for transfers between devices: none -> 54.2 us  [swap(): return lax.ppermute(array, axis, [(i, i ^ bits) for i in range(size)])]
    all_to_all x2 -> x0, blocking collectives: 41.8 us -> none  [from_everyone(): lax.all_to_all(jnp.broadcast_to(array[None], (size, *array.shape)), axis,...]
    all_to_all x10 -> x0, starting transfers between devices: 41.7 us -> none  [the longest x6 21.4 us: summed_on_arrival(): lax.all_to_all(tiles, axis, split_axis=0, concat_axis=0, tiled=True)]
    dot_general x9, matrix products: 30.9 us -> 12.6 us  [the longest x3 4.67 us: compute(): guess = jnp.dot(full_users, piece.T, preferred_element_type=F32)]
    another operation x0 -> x32, other arithmetic: none -> 6.51 us  [the longest x19 2.02 us: absolute(): stack = jnp.stack(pieces)]
    broadcast_in_dim x6 -> x0, local copies, waits for them, and re-layouts: 3.75 us -> none  [from_everyone(): jnp.broadcast_to(array[None], (size, *array.shape))]
  transfers between devices with their start and end apart: 10 -> 52, of which waited for: 10 -> 27; matrix products, arithmetic and copies ran while one was open for 7% -> 10% of each run, Pallas kernels for 0% -> 0%
where the time goes in v1:
time: 149 us
  starting transfers between devices  65.5 us (44%)
  waiting for transfers between devices  54.2 us (36%)
  matrix products  12.6 us (8%)
  other arithmetic  10.2 us (7%)
  between operations  3.46 us (2%)
  local copies, waits for them, and re-layouts  2.69 us (2%)
    ppermute x52, starting transfers between devices, swap(): return lax.ppermute(array, axis, [(i, i ^ bits) for i in range(size)])  65.5 us
    ppermute x52, waiting for transfers between devices, swap(): return lax.ppermute(array, axis, [(i, i ^ bits) for i in range(size)])  54.2 us
    dot_general x3, matrix products, compute(): guess = jnp.dot(full_users, piece.T, preferred_element_type=F32)  4.67 us
    dot_general x3, matrix products, compute(): item_sum = jnp.dot(error.T, full_users, preferred_element_type=F32)  4.15 us
    dot_general x3, matrix products, compute(): user_sum = jnp.dot(error, piece, preferred_element_type=F32)  3.74 us
  transfers between devices with their start and end apart: 52, of which 27 were waited for; matrix products, arithmetic and copies ran while one was open for 10% of the time, Pallas kernels for 0%

profile of v1, /device:TPU:0, one launch (start us, length us, event | category | flops | bytes accessed | tf_op | source)
XLA Modules:
  0.0 148.7 jit_solution(9959857827050400685)
XLA Ops:
  1.7 2.1 %collective-permute-start = (bf16[128,256]{1,0:T(8,128)(2,1)S(1)}, bf16[128,256]{1,0:T(8,128)(2,1)S(1)}, u32[]{:S(2)}, u32[]{:S(2)}) collective-permute-start(bf16[128,256]{1,0:T(8,128)(2,1)S(1)} %get-tuple-element.11), channel_id=1, source_target_pairs={{0,1},{1,0},{2,3},{3,2},{4,5},{5,4},{6,7},{7,6},{8,9},{9,8},{10,11... | collective-permute-start | bytes 196616 | tf_op jit(solution)/shard_map/ppermute | solution.py:15
  5.8 4.0 %collective-permute-start.5 = (bf16[128,256]{1,0:T(8,128)(2,1)S(1)}, bf16[128,256]{1,0:T(8,128)(2,1)S(1)}, u32[]{:S(2)}, u32[]{:S(2)}) collective-permute-start(bf16[128,256]{1,0:T(8,128)(2,1)S(1)} %get-tuple-element.9), channel_id=1, source_target_pairs={{0,64},{8,72},{16,80},{24,88},{32,96},{40,104},{48,112},{56,120},{... | collective-permute-start | bytes 196616 | tf_op jit(solution)/shard_map/ppermute | solution.py:15
  13.9 3.1 %collective-permute-start.8 = (bf16[2,128,256]{2,1,0:T(8,128)(2,1)S(1)}, bf16[2,128,256]{2,1,0:T(8,128)(2,1)S(1)}, u32[]{:S(2)}, u32[]{:S(2)}) collective-permute-start(bf16[2,128,256]{2,1,0:T(8,128)(2,1)S(1)} %get-tuple-element.87), channel_id=1, source_target_pairs={{0,48},{8,56},{16,32},{24,40},{32,16},{40,24},{48,0},{56,8},{64,11... | collective-permute-start | bytes 393224 | tf_op jit(solution)/shard_map/ppermute | solution.py:15
  18.2 2.8 %collective-permute-start.4 = (bf16[2,128,256]{2,1,0:T(8,128)(2,1)S(1)}, bf16[2,128,256]{2,1,0:T(8,128)(2,1)S(1)}, u32[]{:S(2)}, u32[]{:S(2)}) collective-permute-start(bf16[2,128,256]{2,1,0:T(8,128)(2,1)S(1)} %get-tuple-element.91), channel_id=1, source_target_pairs={{0,6},{1,7},{2,4},{3,5},{4,2},{5,3},{6,0},{7,1},{8,14},{9,15},{10,... | collective-permute-start | bytes 393224 | tf_op jit(solution)/shard_map/ppermute | solution.py:15
  21.8 3.0 %collective-permute-start.3 = (bf16[2,128,256]{2,1,0:T(8,128)(2,1)S(1)}, bf16[2,128,256]{2,1,0:T(8,128)(2,1)S(1)}, u32[]{:S(2)}, u32[]{:S(2)}) collective-permute-start(bf16[2,128,256]{2,1,0:T(8,128)(2,1)S(1)} %get-tuple-element.91), channel_id=1, source_target_pairs={{0,4},{1,5},{2,6},{3,7},{4,0},{5,1},{6,2},{7,3},{8,12},{9,13},{10,... | collective-permute-start | bytes 393224 | tf_op jit(solution)/shard_map/ppermute | solution.py:15
  26.1 3.5 %collective-permute-done.3 = bf16[2,128,256]{2,1,0:T(8,128)(2,1)S(1)} collective-permute-done((bf16[2,128,256]{2,1,0:T(8,128)(2,1)S(1)}, bf16[2,128,256]{2,1,0:T(8,128)(2,1)S(1)}, u32[]{:S(2)}, u32[]{:S(2)}) %collective-permute-start.3) | collective-permute-done | bytes 131104 | tf_op jit(solution)/shard_map/ppermute | solution.py:15
  36.7 4.2 %collective-permute-start.21 = (bf16[2,128,256]{2,1,0:T(8,128)(2,1)S(1)}, bf16[2,128,256]{2,1,0:T(8,128)(2,1)S(1)}, u32[]{:S(2)}, u32[]{:S(2)}) collective-permute-start(bf16[2,128,256]{2,1,0:T(8,128)(2,1)S(1)} %get-tuple-element.55), channel_id=1, source_target_pairs={{0,48},{8,56},{16,32},{24,40},{32,16},{40,24},{48,0},{56,8},{64,11... | collective-permute-start | bytes 393224 | tf_op jit(solution)/shard_map/ppermute | solution.py:15
  42.0 4.8 %collective-permute-done.21 = bf16[2,128,256]{2,1,0:T(8,128)(2,1)S(1)} collective-permute-done((bf16[2,128,256]{2,1,0:T(8,128)(2,1)S(1)}, bf16[2,128,256]{2,1,0:T(8,128)(2,1)S(1)}, u32[]{:S(2)}, u32[]{:S(2)}) %collective-permute-start.21) | collective-permute-done | bytes 131104 | tf_op jit(solution)/shard_map/ppermute | solution.py:15
  52.1 2.2 %collective-permute-start.11 = (bf16[2,128,256]{2,1,0:T(8,128)(2,1)S(1)}, bf16[2,128,256]{2,1,0:T(8,128)(2,1)S(1)}, u32[]{:S(2)}, u32[]{:S(2)}) collective-permute-start(bf16[2,128,256]{2,1,0:T(8,128)(2,1)S(1)} %get-tuple-element.63), channel_id=1, source_target_pairs={{0,4},{1,5},{2,6},{3,7},{4,0},{5,1},{6,2},{7,3},{8,12},{9,13},{10,... | collective-permute-start | bytes 393224 | tf_op jit(solution)/shard_map/ppermute | solution.py:15
  55.5 2.3 %collective-permute-start.25 = (bf16[2,128,256]{2,1,0:T(8,128)(2,1)S(1)}, bf16[2,128,256]{2,1,0:T(8,128)(2,1)S(1)}, u32[]{:S(2)}, u32[]{:S(2)}) collective-permute-start(bf16[2,128,256]{2,1,0:T(8,128)(2,1)S(1)} %fusion.57), channel_id=1, source_target_pairs={{0,48},{8,56},{16,32},{24,40},{32,16},{40,24},{48,0},{56,8},{64,11... | collective-permute-start | bytes 393224 | tf_op jit(solution)/shard_map/ppermute | solution.py:15
  66.3 2.2 %collective-permute-start.15 = (bf16[2,128,256]{2,1,0:T(8,128)(2,1)S(1)}, bf16[2,128,256]{2,1,0:T(8,128)(2,1)S(1)}, u32[]{:S(2)}, u32[]{:S(2)}) collective-permute-start(bf16[2,128,256]{2,1,0:T(8,128)(2,1)S(1)} %fusion.56), channel_id=1, source_target_pairs={{0,4},{1,5},{2,6},{3,7},{4,0},{5,1},{6,2},{7,3},{8,12},{9,13},{10,... | collective-permute-start | bytes 393224 | tf_op jit(solution)/shard_map/ppermute | solution.py:15
  69.1 5.6 %collective-permute-done.16 = bf16[2,128,256]{2,1,0:T(8,128)(2,1)S(1)} collective-permute-done((bf16[2,128,256]{2,1,0:T(8,128)(2,1)S(1)}, bf16[2,128,256]{2,1,0:T(8,128)(2,1)S(1)}, u32[]{:S(2)}, u32[]{:S(2)}) %collective-permute-start.16) | collective-permute-done | bytes 131104 | tf_op jit(solution)/shard_map/ppermute | solution.py:15
  81.4 2.0 %collective-permute-start.34 = (bf16[2,128,256]{2,1,0:T(8,128)(2,1)S(1)}, bf16[2,128,256]{2,1,0:T(8,128)(2,1)S(1)}, u32[]{:S(2)}, u32[]{:S(2)}) collective-permute-start(bf16[2,128,256]{2,1,0:T(8,128)(2,1)S(1)} %get-tuple-element.43), channel_id=1, source_target_pairs={{0,48},{8,56},{16,32},{24,40},{32,16},{40,24},{48,0},{56,8},{64,11... | collective-permute-start | bytes 393224 | tf_op jit(solution)/shard_map/ppermute | solution.py:15
  85.6 5.2 %collective-permute-done.34 = bf16[2,128,256]{2,1,0:T(8,128)(2,1)S(1)} collective-permute-done((bf16[2,128,256]{2,1,0:T(8,128)(2,1)S(1)}, bf16[2,128,256]{2,1,0:T(8,128)(2,1)S(1)}, u32[]{:S(2)}, u32[]{:S(2)}) %collective-permute-start.34) | collective-permute-done | bytes 131104 | tf_op jit(solution)/shard_map/ppermute | solution.py:15
  91.8 2.8 %collective-permute-start.35 = (bf16[2,128,256]{2,1,0:T(8,128)(2,1)S(1)}, bf16[2,128,256]{2,1,0:T(8,128)(2,1)S(1)}, u32[]{:S(2)}, u32[]{:S(2)}) collective-permute-start(bf16[2,128,256]{2,1,0:T(8,128)(2,1)S(1)} %fusion.23), channel_id=1, source_target_pairs={{0,64},{8,72},{16,80},{24,88},{32,96},{40,104},{48,112},{56,120},{... | collective-permute-start | bytes 393224 | tf_op jit(solution)/shard_map/ppermute | solution.py:15
  97.0 2.2 %collective-permute-start.28 = (bf16[2,128,256]{2,1,0:T(8,128)(2,1)S(1)}, bf16[2,128,256]{2,1,0:T(8,128)(2,1)S(1)}, u32[]{:S(2)}, u32[]{:S(2)}) collective-permute-start(bf16[2,128,256]{2,1,0:T(8,128)(2,1)S(1)} %get-tuple-element.47), channel_id=1, source_target_pairs={{0,4},{1,5},{2,6},{3,7},{4,0},{5,1},{6,2},{7,3},{8,12},{9,13},{10,... | collective-permute-start | bytes 393224 | tf_op jit(solution)/shard_map/ppermute | solution.py:15
  100.2 2.4 %collective-permute-start.41 = (bf16[2,128,256]{2,1,0:T(8,128)(2,1)S(1)}, bf16[2,128,256]{2,1,0:T(8,128)(2,1)S(1)}, u32[]{:S(2)}, u32[]{:S(2)}) collective-permute-start(bf16[2,128,256]{2,1,0:T(8,128)(2,1)S(1)} %get-tuple-element.4), channel_id=1, source_target_pairs={{0,48},{8,56},{16,32},{24,40},{32,16},{40,24},{48,0},{56,8},{64,11... | collective-permute-start | bytes 393224 | tf_op jit(solution)/shard_map/ppermute | solution.py:15
  105.0 2.1 %collective-permute-done.41 = bf16[2,128,256]{2,1,0:T(8,128)(2,1)S(1)} collective-permute-done((bf16[2,128,256]{2,1,0:T(8,128)(2,1)S(1)}, bf16[2,128,256]{2,1,0:T(8,128)(2,1)S(1)}, u32[]{:S(2)}, u32[]{:S(2)}) %collective-permute-start.41) | collective-permute-done | bytes 131104 | tf_op jit(solution)/shard_map/ppermute | solution.py:15
  111.2 2.2 %collective-permute-start.37 = (bf16[2,128,256]{2,1,0:T(8,128)(2,1)S(1)}, bf16[2,128,256]{2,1,0:T(8,128)(2,1)S(1)}, u32[]{:S(2)}, u32[]{:S(2)}) collective-permute-start(bf16[2,128,256]{2,1,0:T(8,128)(2,1)S(1)} %get-tuple-element.6), channel_id=1, source_target_pairs={{0,4},{1,5},{2,6},{3,7},{4,0},{5,1},{6,2},{7,3},{8,12},{9,13},{10,... | collective-permute-start | bytes 393224 | tf_op jit(solution)/shard_map/ppermute | solution.py:15
  115.6 3.9 %collective-permute-done.38 = bf16[2,128,256]{2,1,0:T(8,128)(2,1)S(1)} collective-permute-done((bf16[2,128,256]{2,1,0:T(8,128)(2,1)S(1)}, bf16[2,128,256]{2,1,0:T(8,128)(2,1)S(1)}, u32[]{:S(2)}, u32[]{:S(2)}) %collective-permute-start.38) | collective-permute-done | bytes 131104 | tf_op jit(solution)/shard_map/ppermute | solution.py:15
  131.3 2.4 %collective-permute-start.50 = (bf16[2,128,256]{2,1,0:T(8,128)(2,1)S(1)}, bf16[2,128,256]{2,1,0:T(8,128)(2,1)S(1)}, u32[]{:S(2)}, u32[]{:S(2)}) collective-permute-start(bf16[2,128,256]{2,1,0:T(8,128)(2,1)S(1)} %get-tuple-element.27), channel_id=1, source_target_pairs={{0,48},{8,56},{16,32},{24,40},{32,16},{40,24},{48,0},{56,8},{64,11... | collective-permute-start | bytes 393224 | tf_op jit(solution)/shard_map/ppermute | solution.py:15
  134.2 2.7 %collective-permute-done.45 = bf16[2,128,256]{2,1,0:T(8,128)(2,1)S(1)} collective-permute-done((bf16[2,128,256]{2,1,0:T(8,128)(2,1)S(1)}, bf16[2,128,256]{2,1,0:T(8,128)(2,1)S(1)}, u32[]{:S(2)}, u32[]{:S(2)}) %collective-permute-start.45) | collective-permute-done | bytes 131104 | tf_op jit(solution)/shard_map/ppermute | solution.py:15
  137.9 2.5 %collective-permute-done.50 = bf16[2,128,256]{2,1,0:T(8,128)(2,1)S(1)} collective-permute-done((bf16[2,128,256]{2,1,0:T(8,128)(2,1)S(1)}, bf16[2,128,256]{2,1,0:T(8,128)(2,1)S(1)}, u32[]{:S(2)}, u32[]{:S(2)}) %collective-permute-start.50) | collective-permute-done | bytes 131104 | tf_op jit(solution)/shard_map/ppermute | solution.py:15
  143.9 4.0 %collective-permute-done.51 = bf16[128,256]{1,0:T(8,128)(2,1)S(1)} collective-permute-done((bf16[128,256]{1,0:T(8,128)(2,1)S(1)}, bf16[128,256]{1,0:T(8,128)(2,1)S(1)}, u32[]{:S(2)}, u32[]{:S(2)}) %collective-permute-start.51) | collective-permute-done | bytes 65568 | tf_op jit(solution)/shard_map/ppermute | solution.py:15
  (178 shorter events, 70.8 us)
Async XLA Ops:
  1.7 15.9 %collective-permute-start = (bf16[128,256]{1,0:T(8,128)(2,1)S(1)}, bf16[128,256]{1,0:T(8,128)(2,1)S(1)}, u32[]{:S(2)}, u32[]{:S(2)}) collective-permute-start(bf16[128,256]{1,0:T(8,128)(2,1)S(1)} %get-tuple-element.11), channel_id=1, source_target_pairs={{0,1},{1,0},{2,3},{3,2},{4,5},{5,4},{6,7},{7,6},{8,9},{9,8},{10,11... | collective-permute-start | bytes 196616 | tf_op jit(solution)/shard_map/ppermute | solution.py:15
  4.7 13.5 %collective-permute-start.1 = (bf16[2,128,256]{2,1,0:T(8,128)(2,1)S(1)}, bf16[2,128,256]{2,1,0:T(8,128)(2,1)S(1)}, u32[]{:S(2)}, u32[]{:S(2)}) collective-permute-start(bf16[2,128,256]{2,1,0:T(8,128)(2,1)S(1)} %pad_maximum_fusion.15), channel_id=1, source_target_pairs={{0,1},{1,0},{2,3},{3,2},{4,5},{5,4},{6,7},{7,6},{8,9},{9,8},{10,11... | collective-permute-start | bytes 393224 | tf_op jit(solution)/shard_map/ppermute | solution.py:15
  5.8 8.0 %collective-permute-start.5 = (bf16[128,256]{1,0:T(8,128)(2,1)S(1)}, bf16[128,256]{1,0:T(8,128)(2,1)S(1)}, u32[]{:S(2)}, u32[]{:S(2)}) collective-permute-start(bf16[128,256]{1,0:T(8,128)(2,1)S(1)} %get-tuple-element.9), channel_id=1, source_target_pairs={{0,64},{8,72},{16,80},{24,88},{32,96},{40,104},{48,112},{56,120},{... | collective-permute-start | bytes 196616 | tf_op jit(solution)/shard_map/ppermute | solution.py:15
  10.8 23.9 %collective-permute-start.17 = (bf16[2,128,256]{2,1,0:T(8,128)(2,1)S(1)}, bf16[2,128,256]{2,1,0:T(8,128)(2,1)S(1)}, u32[]{:S(2)}, u32[]{:S(2)}) collective-permute-start(bf16[2,128,256]{2,1,0:T(8,128)(2,1)S(1)} %pad_maximum_fusion.18), channel_id=1, source_target_pairs={{0,64},{8,72},{16,80},{24,88},{32,96},{40,104},{48,112},{56,120},{... | collective-permute-start | bytes 393224 | tf_op jit(solution)/shard_map/ppermute | solution.py:15
  13.9 7.9 %collective-permute-start.8 = (bf16[2,128,256]{2,1,0:T(8,128)(2,1)S(1)}, bf16[2,128,256]{2,1,0:T(8,128)(2,1)S(1)}, u32[]{:S(2)}, u32[]{:S(2)}) collective-permute-start(bf16[2,128,256]{2,1,0:T(8,128)(2,1)S(1)} %get-tuple-element.87), channel_id=1, source_target_pairs={{0,48},{8,56},{16,32},{24,40},{32,16},{40,24},{48,0},{56,8},{64,11... | collective-permute-start | bytes 393224 | tf_op jit(solution)/shard_map/ppermute | solution.py:15
  17.0 7.8 %collective-permute-start.7 = (bf16[2,128,256]{2,1,0:T(8,128)(2,1)S(1)}, bf16[2,128,256]{2,1,0:T(8,128)(2,1)S(1)}, u32[]{:S(2)}, u32[]{:S(2)}) collective-permute-start(bf16[2,128,256]{2,1,0:T(8,128)(2,1)S(1)} %get-tuple-element.87), channel_id=1, source_target_pairs={{0,32},{8,40},{16,48},{24,56},{32,0},{40,8},{48,16},{56,24},{64,96... | collective-permute-start | bytes 393224 | tf_op jit(solution)/shard_map/ppermute | solution.py:15
  17.6 8.0 %collective-permute-start.6 = (bf16[2,128,256]{2,1,0:T(8,128)(2,1)S(1)}, bf16[2,128,256]{2,1,0:T(8,128)(2,1)S(1)}, u32[]{:S(2)}, u32[]{:S(2)}) collective-permute-start(bf16[2,128,256]{2,1,0:T(8,128)(2,1)S(1)} %get-tuple-element.87), channel_id=1, source_target_pairs={{0,16},{8,24},{16,0},{24,8},{32,48},{40,56},{48,32},{56,40},{64,80... | collective-permute-start | bytes 393224 | tf_op jit(solution)/shard_map/ppermute | solution.py:15
  18.2 7.9 %collective-permute-start.4 = (bf16[2,128,256]{2,1,0:T(8,128)(2,1)S(1)}, bf16[2,128,256]{2,1,0:T(8,128)(2,1)S(1)}, u32[]{:S(2)}, u32[]{:S(2)}) collective-permute-start(bf16[2,128,256]{2,1,0:T(8,128)(2,1)S(1)} %get-tuple-element.91), channel_id=1, source_target_pairs={{0,6},{1,7},{2,4},{3,5},{4,2},{5,3},{6,0},{7,1},{8,14},{9,15},{10,... | collective-permute-start | bytes 393224 | tf_op jit(solution)/shard_map/ppermute | solution.py:15
  36.7 10.1 %collective-permute-start.21 = (bf16[2,128,256]{2,1,0:T(8,128)(2,1)S(1)}, bf16[2,128,256]{2,1,0:T(8,128)(2,1)S(1)}, u32[]{:S(2)}, u32[]{:S(2)}) collective-permute-start(bf16[2,128,256]{2,1,0:T(8,128)(2,1)S(1)} %get-tuple-element.55), channel_id=1, source_target_pairs={{0,48},{8,56},{16,32},{24,40},{32,16},{40,24},{48,0},{56,8},{64,11... | collective-permute-start | bytes 393224 | tf_op jit(solution)/shard_map/ppermute | solution.py:15
  40.9 7.9 %collective-permute-start.20 = (bf16[2,128,256]{2,1,0:T(8,128)(2,1)S(1)}, bf16[2,128,256]{2,1,0:T(8,128)(2,1)S(1)}, u32[]{:S(2)}, u32[]{:S(2)}) collective-permute-start(bf16[2,128,256]{2,1,0:T(8,128)(2,1)S(1)} %get-tuple-element.56), channel_id=1, source_target_pairs={{0,32},{8,40},{16,48},{24,56},{32,0},{40,8},{48,16},{56,24},{64,96... | collective-permute-start | bytes 393224 | tf_op jit(solution)/shard_map/ppermute | solution.py:15
  40.9 7.9 %collective-permute-start.19 = (bf16[2,128,256]{2,1,0:T(8,128)(2,1)S(1)}, bf16[2,128,256]{2,1,0:T(8,128)(2,1)S(1)}, u32[]{:S(2)}, u32[]{:S(2)}) collective-permute-start(bf16[2,128,256]{2,1,0:T(8,128)(2,1)S(1)} %get-tuple-element.54), channel_id=1, source_target_pairs={{0,16},{8,24},{16,0},{24,8},{32,48},{40,56},{48,32},{56,40},{64,80... | collective-permute-start | bytes 393224 | tf_op jit(solution)/shard_map/ppermute | solution.py:15
  50.8 8.0 %collective-permute-start.12 = (bf16[2,128,256]{2,1,0:T(8,128)(2,1)S(1)}, bf16[2,128,256]{2,1,0:T(8,128)(2,1)S(1)}, u32[]{:S(2)}, u32[]{:S(2)}) collective-permute-start(bf16[2,128,256]{2,1,0:T(8,128)(2,1)S(1)} %get-tuple-element.62), channel_id=1, source_target_pairs={{0,6},{1,7},{2,4},{3,5},{4,2},{5,3},{6,0},{7,1},{8,14},{9,15},{10,... | collective-permute-start | bytes 393224 | tf_op jit(solution)/shard_map/ppermute | solution.py:15
  64.6 11.0 %collective-permute-start.26 = (bf16[4,2,128,256]{3,2,1,0:T(8,128)(2,1)S(1)}, bf16[4,2,128,256]{3,2,1,0:T(8,128)(2,1)S(1)}, u32[]{:S(2)}, u32[]{:S(2)}) collective-permute-start(bf16[4,2,128,256]{3,2,1,0:T(8,128)(2,1)S(1)} %get-tuple-element.48), channel_id=1, source_target_pairs={{0,8},{8,0},{16,24},{24,16},{32,40},{40,32},{48,56},{56,48},{64,72... | collective-permute-start | bytes 1572872 | tf_op jit(solution)/shard_map/ppermute | solution.py:15
  65.0 9.8 %collective-permute-start.16 = (bf16[2,128,256]{2,1,0:T(8,128)(2,1)S(1)}, bf16[2,128,256]{2,1,0:T(8,128)(2,1)S(1)}, u32[]{:S(2)}, u32[]{:S(2)}) collective-permute-start(bf16[2,128,256]{2,1,0:T(8,128)(2,1)S(1)} %fusion.56), channel_id=1, source_target_pairs={{0,6},{1,7},{2,4},{3,5},{4,2},{5,3},{6,0},{7,1},{8,14},{9,15},{10,... | collective-permute-start | bytes 393224 | tf_op jit(solution)/shard_map/ppermute | solution.py:15
  66.3 8.5 %collective-permute-start.15 = (bf16[2,128,256]{2,1,0:T(8,128)(2,1)S(1)}, bf16[2,128,256]{2,1,0:T(8,128)(2,1)S(1)}, u32[]{:S(2)}, u32[]{:S(2)}) collective-permute-start(bf16[2,128,256]{2,1,0:T(8,128)(2,1)S(1)} %fusion.56), channel_id=1, source_target_pairs={{0,4},{1,5},{2,6},{3,7},{4,0},{5,1},{6,2},{7,3},{8,12},{9,13},{10,... | collective-permute-start | bytes 393224 | tf_op jit(solution)/shard_map/ppermute | solution.py:15
  81.4 9.3 %collective-permute-start.34 = (bf16[2,128,256]{2,1,0:T(8,128)(2,1)S(1)}, bf16[2,128,256]{2,1,0:T(8,128)(2,1)S(1)}, u32[]{:S(2)}, u32[]{:S(2)}) collective-permute-start(bf16[2,128,256]{2,1,0:T(8,128)(2,1)S(1)} %get-tuple-element.43), channel_id=1, source_target_pairs={{0,48},{8,56},{16,32},{24,40},{32,16},{40,24},{48,0},{56,8},{64,11... | collective-permute-start | bytes 393224 | tf_op jit(solution)/shard_map/ppermute | solution.py:15
  83.5 7.9 %collective-permute-start.33 = (bf16[2,128,256]{2,1,0:T(8,128)(2,1)S(1)}, bf16[2,128,256]{2,1,0:T(8,128)(2,1)S(1)}, u32[]{:S(2)}, u32[]{:S(2)}) collective-permute-start(bf16[2,128,256]{2,1,0:T(8,128)(2,1)S(1)} %get-tuple-element.44), channel_id=1, source_target_pairs={{0,32},{8,40},{16,48},{24,56},{32,0},{40,8},{48,16},{56,24},{64,96... | collective-permute-start | bytes 393224 | tf_op jit(solution)/shard_map/ppermute | solution.py:15
  91.8 8.3 %collective-permute-start.35 = (bf16[2,128,256]{2,1,0:T(8,128)(2,1)S(1)}, bf16[2,128,256]{2,1,0:T(8,128)(2,1)S(1)}, u32[]{:S(2)}, u32[]{:S(2)}) collective-permute-start(bf16[2,128,256]{2,1,0:T(8,128)(2,1)S(1)} %fusion.23), channel_id=1, source_target_pairs={{0,64},{8,72},{16,80},{24,88},{32,96},{40,104},{48,112},{56,120},{... | collective-permute-start | bytes 393224 | tf_op jit(solution)/shard_map/ppermute | solution.py:15
  109.3 11.1 %collective-permute-start.42 = (bf16[4,2,128,256]{3,2,1,0:T(8,128)(2,1)S(1)}, bf16[4,2,128,256]{3,2,1,0:T(8,128)(2,1)S(1)}, u32[]{:S(2)}, u32[]{:S(2)}) collective-permute-start(bf16[4,2,128,256]{3,2,1,0:T(8,128)(2,1)S(1)} %get-tuple-element.32), channel_id=1, source_target_pairs={{0,8},{8,0},{16,24},{24,16},{32,40},{40,32},{48,56},{56,48},{64,72... | collective-permute-start | bytes 1572872 | tf_op jit(solution)/shard_map/ppermute | solution.py:15
  110.1 9.4 %collective-permute-start.38 = (bf16[2,128,256]{2,1,0:T(8,128)(2,1)S(1)}, bf16[2,128,256]{2,1,0:T(8,128)(2,1)S(1)}, u32[]{:S(2)}, u32[]{:S(2)}) collective-permute-start(bf16[2,128,256]{2,1,0:T(8,128)(2,1)S(1)} %get-tuple-element.6), channel_id=1, source_target_pairs={{0,6},{1,7},{2,4},{3,5},{4,2},{5,3},{6,0},{7,1},{8,14},{9,15},{10,... | collective-permute-start | bytes 393224 | tf_op jit(solution)/shard_map/ppermute | solution.py:15
  111.2 8.3 %collective-permute-start.37 = (bf16[2,128,256]{2,1,0:T(8,128)(2,1)S(1)}, bf16[2,128,256]{2,1,0:T(8,128)(2,1)S(1)}, u32[]{:S(2)}, u32[]{:S(2)}) collective-permute-start(bf16[2,128,256]{2,1,0:T(8,128)(2,1)S(1)} %get-tuple-element.6), channel_id=1, source_target_pairs={{0,4},{1,5},{2,6},{3,7},{4,0},{5,1},{6,2},{7,3},{8,12},{9,13},{10,... | collective-permute-start | bytes 393224 | tf_op jit(solution)/shard_map/ppermute | solution.py:15
  126.9 10.0 %collective-permute-start.45 = (bf16[2,128,256]{2,1,0:T(8,128)(2,1)S(1)}, bf16[2,128,256]{2,1,0:T(8,128)(2,1)S(1)}, u32[]{:S(2)}, u32[]{:S(2)}) collective-permute-start(bf16[2,128,256]{2,1,0:T(8,128)(2,1)S(1)} %get-tuple-element.30), channel_id=1, source_target_pairs={{0,6},{1,7},{2,4},{3,5},{4,2},{5,3},{6,0},{7,1},{8,14},{9,15},{10,... | collective-permute-start | bytes 393224 | tf_op jit(solution)/shard_map/ppermute | solution.py:15
  128.2 9.5 %collective-permute-start.44 = (bf16[2,128,256]{2,1,0:T(8,128)(2,1)S(1)}, bf16[2,128,256]{2,1,0:T(8,128)(2,1)S(1)}, u32[]{:S(2)}, u32[]{:S(2)}) collective-permute-start(bf16[2,128,256]{2,1,0:T(8,128)(2,1)S(1)} %get-tuple-element.31), channel_id=1, source_target_pairs={{0,4},{1,5},{2,6},{3,7},{4,0},{5,1},{6,2},{7,3},{8,12},{9,13},{10,... | collective-permute-start | bytes 393224 | tf_op jit(solution)/shard_map/ppermute | solution.py:15
  131.3 9.2 %collective-permute-start.50 = (bf16[2,128,256]{2,1,0:T(8,128)(2,1)S(1)}, bf16[2,128,256]{2,1,0:T(8,128)(2,1)S(1)}, u32[]{:S(2)}, u32[]{:S(2)}) collective-permute-start(bf16[2,128,256]{2,1,0:T(8,128)(2,1)S(1)} %get-tuple-element.27), channel_id=1, source_target_pairs={{0,48},{8,56},{16,32},{24,40},{32,16},{40,24},{48,0},{56,8},{64,11... | collective-permute-start | bytes 393224 | tf_op jit(solution)/shard_map/ppermute | solution.py:15
  (34 other events, 218.9 us)

commit v2 on v1

--- a/solution.py
+++ b/solution.py
@@ -13,6 +13,10 @@
 def swap(array, axis, bits):
     size = lax.axis_size(axis)
     return lax.ppermute(array, axis, [(i, i ^ bits) for i in range(size)])
+
+
+def after(value, *others):
+    return lax.optimization_barrier((value, others))[0]
 
 
 def pick(array, index):
@@ -34,36 +38,40 @@
     colmask = jnp.repeat(tile_mask, BLK, axis=1).astype(F32)
     alive = (jnp.arange(rows, dtype=jnp.int32) < counts[0]).astype(F32)
 
-    def compute(full_users, piece):
+    def errors(full_users, piece):
         guess = jnp.dot(full_users, piece.T, preferred_element_type=F32)
         error = (ratings.astype(F32) - guess).reshape(rows // BLK, BLK, cols) * colmask[:, None, :]
-        error = (error.reshape(rows, cols) * alive[:, None]).astype(BF)
-        user_sum = jnp.dot(error, piece, preferred_element_type=F32)
-        item_sum = jnp.dot(error.T, full_users, preferred_element_type=F32)
+        return (error.reshape(rows, cols) * alive[:, None]).astype(BF)
+
+    def gather(user_pair, item_pair):
+        got_v = [swap(item_pair, "usr", 2 * k) for k in (2, 1, 3)]
+        got_u = [swap(user_pair, "itm", 2 * k) for k in (2, 1, 3)]
+        first = got_u[0]
+        got_v = after(got_v, first)
+        half = absolute([item_pair, got_v[1], got_v[0], got_v[2]], y)
+        other = swap(half, "usr", 1)
+        full_users = absolute([user_pair, got_u[1], got_u[0], got_u[2]], x).reshape(rows, K)
+        both = absolute([half, after(other, full_users)], c)
+        return full_users, both.transpose(2, 1, 0, 3, 4).reshape(cols, K)
+
+    def reduce(error, full_users, piece):
+        part = jnp.dot(error.T, full_users, preferred_element_type=F32).astype(BF)
+        part = part.reshape(2, 4, 2, BLK, K).transpose(2, 1, 0, 3, 4)
+        other = swap(pick(part, 1 - c), "usr", 1)
+        user_part = jnp.dot(after(error, part), piece, preferred_element_type=F32).astype(BF)
+        user_part = user_part.reshape(4, 2, BLK, K)
+        other, user_part = lax.optimization_barrier((other, user_part))
+        half = (pick(part, c).astype(F32) + other.astype(F32)).astype(BF)
+        got_v = [swap(pick(half, y ^ k), "usr", 2 * k) for k in (2, 1, 3)]
+        got_u = [swap(pick(user_part, x ^ k), "itm", 2 * k) for k in (2, 1, 3)]
+        got_v = after(got_v, got_u[0])
+        item_sum = pick(half, y).astype(F32)
+        for got in got_v:
+            item_sum += got.astype(F32)
+        user_sum = pick(user_part, x).astype(F32)
+        for got in got_u:
+            user_sum += got.astype(F32)
         return user_sum.astype(BF), item_sum.astype(BF)
-
-    def gather_users(pair):
-        pieces = [pair] + [swap(pair, "itm", 2 * k) for k in (1, 2, 3)]
-        return absolute(pieces, x).reshape(rows, K)
-
-    def gather_items(pair):
-        pieces = [pair] + [swap(pair, "usr", 2 * k) for k in (1, 2, 3)]
-        half = absolute(pieces, y)
-        other = swap(half, "usr", 1)
-        both = absolute([half, other], c)
-        return both.transpose(2, 1, 0, 3, 4).reshape(cols, K)
-
-    def reduce_users(part):
-        part = part.reshape(4, 2, BLK, K)
-        got = [swap(pick(part, x ^ k), "itm", 2 * k).astype(F32) for k in (1, 2, 3)]
-        return (pick(part, x).astype(F32) + got[0] + got[1] + got[2]).astype(BF)
-
-    def reduce_items(part):
-        part = part.reshape(2, 4, 2, BLK, K).transpose(2, 1, 0, 3, 4)
-        half = pick(part, c).astype(F32) + swap(pick(part, 1 - c), "usr", 1).astype(F32)
-        half = half.astype(BF)
-        got = [swap(pick(half, y ^ k), "usr", 2 * k).astype(F32) for k in (1, 2, 3)]
-        return (pick(half, y).astype(F32) + got[0] + got[1] + got[2]).astype(BF)
 
     def pair_of(mine, other, z):
         return absolute([mine, other], z)
@@ -84,8 +92,8 @@
 
     half_step = 0.5 * step_size
     for leap in range(LEAPS):
-        gu, gv = compute(gather_users(user_bf), gather_items(item_bf))
-        su, sv = reduce_users(gu), reduce_items(gv)
+        full_users, piece = gather(user_bf, item_bf)
+        su, sv = reduce(errors(full_users, piece), full_users, piece)
         eu = su.astype(F32) + swap(su, "itm", 1).astype(F32)
         ev = sv.astype(F32) + swap(sv, "usr", 8).astype(F32)
         scale = half_step if leap == 0 else 2 * half_step
@@ -94,8 +102,8 @@
         up = up + step_size * um
         vp = vp + step_size * vm
         user_bf, item_bf = up.astype(BF), vp.astype(BF)
-    gu, gv = compute(gather_users(user_bf), gather_items(item_bf))
-    su, sv = reduce_users(gu), reduce_items(gv)
+    full_users, piece = gather(user_bf, item_bf)
+    su, sv = reduce(errors(full_users, piece), full_users, piece)
     eu = pick(su, zl).astype(F32) + swap(pick(su, 1 - zl), "itm", 1).astype(F32)
     ev = pick(sv, zh).astype(F32) + swap(pick(sv, 1 - zh), "usr", 8).astype(F32)
     up, vp, um, vm = pick(up, zl), pick(vp, zh), pick(um, zl), pick(vm, zh)

time: 149 us -> 143 us (0.960)
  waiting for transfers between devices: 54.2 us -> 42.1 us
  starting transfers between devices: 65.5 us -> 72 us
    ppermute x52, waiting for transfers between devices: 54.2 us -> 42.1 us  [swap(): return lax.ppermute(array, axis, [(i, i ^ bits) for i in range(size)])]
    ppermute x52, starting transfers between devices: 65.5 us -> 72 us  [swap(): return lax.ppermute(array, axis, [(i, i ^ bits) for i in range(size)])]
  transfers between devices with their start and end apart: 52 -> 52, of which waited for: 27 -> 29; matrix products, arithmetic and copies ran while one was open for 10% -> 8% of each run, Pallas kernels for 0% -> 0%
where the time goes in v2:
time: 143 us; the launch traced here: 142 us
  starting transfers between devices  72 us (50%)
  waiting for transfers between devices  42.1 us (29%)
  matrix products  12.6 us (9%)
  other arithmetic  10.3 us (7%)
  between operations  3.5 us (2%)
  local copies, waits for them, and re-layouts  1.86 us (1%)
    ppermute x52, starting transfers between devices, swap(): return lax.ppermute(array, axis, [(i, i ^ bits) for i in range(size)])  72 us
    ppermute x52, waiting for transfers between devices, swap(): return lax.ppermute(array, axis, [(i, i ^ bits) for i in range(size)])  42.1 us
    dot_general x3, matrix products, errors(): guess = jnp.dot(full_users, piece.T, preferred_element_type=F32)  4.67 us
    dot_general x3, matrix products, reduce(): part = jnp.dot(error.T, full_users, preferred_element_type=F32).astype(BF)  4.14 us
    dot_general x3, matrix products, reduce(): jnp.dot(after(error, part), piece, preferred_element_type=F32).astype(BF)  3.74 us
  transfers between devices with their start and end apart: 52, of which 29 were waited for; matrix products, arithmetic and copies ran while one was open for 8% of the time, Pallas kernels for 0%

profile of v2, /device:TPU:0, one launch (start us, length us, event | category | flops | bytes accessed | tf_op | source)
XLA Modules:
  0.0 142.3 jit_solution(5408146131569579982)
XLA Ops:
  1.7 4.0 %collective-permute-start.5 = (bf16[128,256]{1,0:T(8,128)(2,1)S(1)}, bf16[128,256]{1,0:T(8,128)(2,1)S(1)}, u32[]{:S(2)}, u32[]{:S(2)}) collective-permute-start(bf16[128,256]{1,0:T(8,128)(2,1)S(1)} %get-tuple-element.63), channel_id=1, source_target_pairs={{0,64},{8,72},{16,80},{24,88},{32,96},{40,104},{48,112},{56,120},{... | collective-permute-start | bytes 196616 | tf_op jit(solution)/shard_map/ppermute | solution.py:15
  12.9 3.3 %collective-permute-start.6 = (bf16[2,128,256]{2,1,0:T(8,128)(2,1)S(1)}, bf16[2,128,256]{2,1,0:T(8,128)(2,1)S(1)}, u32[]{:S(2)}, u32[]{:S(2)}) collective-permute-start(bf16[2,128,256]{2,1,0:T(8,128)(2,1)S(1)} %get-tuple-element.141), channel_id=1, source_target_pairs={{0,32},{8,40},{16,48},{24,56},{32,0},{40,8},{48,16},{56,24},{64,96... | collective-permute-start | bytes 393224 | tf_op jit(solution)/shard_map/ppermute | solution.py:15
  17.3 3.1 %collective-permute-start.3 = (bf16[2,128,256]{2,1,0:T(8,128)(2,1)S(1)}, bf16[2,128,256]{2,1,0:T(8,128)(2,1)S(1)}, u32[]{:S(2)}, u32[]{:S(2)}) collective-permute-start(bf16[2,128,256]{2,1,0:T(8,128)(2,1)S(1)} %get-tuple-element.145), channel_id=1, source_target_pairs={{0,4},{1,5},{2,6},{3,7},{4,0},{5,1},{6,2},{7,3},{8,12},{9,13},{10,... | collective-permute-start | bytes 393224 | tf_op jit(solution)/shard_map/ppermute | solution.py:15
  21.1 2.5 %collective-permute-start.4 = (bf16[2,128,256]{2,1,0:T(8,128)(2,1)S(1)}, bf16[2,128,256]{2,1,0:T(8,128)(2,1)S(1)}, u32[]{:S(2)}, u32[]{:S(2)}) collective-permute-start(bf16[2,128,256]{2,1,0:T(8,128)(2,1)S(1)} %get-tuple-element.145), channel_id=1, source_target_pairs={{0,6},{1,7},{2,4},{3,5},{4,2},{5,3},{6,0},{7,1},{8,14},{9,15},{10,... | collective-permute-start | bytes 393224 | tf_op jit(solution)/shard_map/ppermute | solution.py:15
  33.4 3.1 %collective-permute-start.19 = (bf16[2,128,256]{2,1,0:T(8,128)(2,1)S(1)}, bf16[2,128,256]{2,1,0:T(8,128)(2,1)S(1)}, u32[]{:S(2)}, u32[]{:S(2)}) collective-permute-start(bf16[2,128,256]{2,1,0:T(8,128)(2,1)S(1)} %get-tuple-element.110), channel_id=1, source_target_pairs={{0,32},{8,40},{16,48},{24,56},{32,0},{40,8},{48,16},{56,24},{64,96... | collective-permute-start | bytes 393224 | tf_op jit(solution)/shard_map/ppermute | solution.py:15
  41.4 2.4 %collective-permute-start.13 = (bf16[2,128,256]{2,1,0:T(8,128)(2,1)S(1)}, bf16[2,128,256]{2,1,0:T(8,128)(2,1)S(1)}, u32[]{:S(2)}, u32[]{:S(2)}) collective-permute-start(bf16[2,128,256]{2,1,0:T(8,128)(2,1)S(1)} %get-tuple-element.116), channel_id=1, source_target_pairs={{0,6},{1,7},{2,4},{3,5},{4,2},{5,3},{6,0},{7,1},{8,14},{9,15},{10,... | collective-permute-start | bytes 393224 | tf_op jit(solution)/shard_map/ppermute | solution.py:15
  43.8 1.9 %collective-permute-done.11 = bf16[2,128,256]{2,1,0:T(8,128)(2,1)S(1)} collective-permute-done((bf16[2,128,256]{2,1,0:T(8,128)(2,1)S(1)}, bf16[2,128,256]{2,1,0:T(8,128)(2,1)S(1)}, u32[]{:S(2)}, u32[]{:S(2)}) %collective-permute-start.11) | collective-permute-done | bytes 131104 | tf_op jit(solution)/shard_map/ppermute | solution.py:15
  45.8 3.9 %collective-permute-start.22 = (bf16[2,128,256]{2,1,0:T(8,128)(2,1)S(1)}, bf16[2,128,256]{2,1,0:T(8,128)(2,1)S(1)}, u32[]{:S(2)}, u32[]{:S(2)}) collective-permute-start(bf16[2,128,256]{2,1,0:T(8,128)(2,1)S(1)} %fusion.29), channel_id=1, source_target_pairs={{0,64},{8,72},{16,80},{24,88},{32,96},{40,104},{48,112},{56,120},{... | collective-permute-start | bytes 393224 | tf_op jit(solution)/shard_map/ppermute | solution.py:15
  49.9 3.8 %collective-permute-done.22 = bf16[2,128,256]{2,1,0:T(8,128)(2,1)S(1)} collective-permute-done((bf16[2,128,256]{2,1,0:T(8,128)(2,1)S(1)}, bf16[2,128,256]{2,1,0:T(8,128)(2,1)S(1)}, u32[]{:S(2)}, u32[]{:S(2)}) %collective-permute-start.22) | collective-permute-done | bytes 131104 | tf_op jit(solution)/shard_map/ppermute | solution.py:15
  53.8 3.3 %collective-permute-start.23 = (bf16[2,128,256]{2,1,0:T(8,128)(2,1)S(1)}, bf16[2,128,256]{2,1,0:T(8,128)(2,1)S(1)}, u32[]{:S(2)}, u32[]{:S(2)}) collective-permute-start(bf16[2,128,256]{2,1,0:T(8,128)(2,1)S(1)} %fusion.57), channel_id=1, source_target_pairs={{0,32},{8,40},{16,48},{24,56},{32,0},{40,8},{48,16},{56,24},{64,96... | collective-permute-start | bytes 393224 | tf_op jit(solution)/shard_map/ppermute | solution.py:15
  65.5 1.9 %collective-permute-start.17 = (bf16[2,128,256]{2,1,0:T(8,128)(2,1)S(1)}, bf16[2,128,256]{2,1,0:T(8,128)(2,1)S(1)}, u32[]{:S(2)}, u32[]{:S(2)}) collective-permute-start(bf16[2,128,256]{2,1,0:T(8,128)(2,1)S(1)} %fusion.56), channel_id=1, source_target_pairs={{0,6},{1,7},{2,4},{3,5},{4,2},{5,3},{6,0},{7,1},{8,14},{9,15},{10,... | collective-permute-start | bytes 393224 | tf_op jit(solution)/shard_map/ppermute | solution.py:15
  67.4 3.6 %collective-permute-done.15 = bf16[2,128,256]{2,1,0:T(8,128)(2,1)S(1)} collective-permute-done((bf16[2,128,256]{2,1,0:T(8,128)(2,1)S(1)}, bf16[2,128,256]{2,1,0:T(8,128)(2,1)S(1)}, u32[]{:S(2)}, u32[]{:S(2)}) %collective-permute-start.15) | collective-permute-done | bytes 131104 | tf_op jit(solution)/shard_map/ppermute | solution.py:15
  78.3 3.1 %collective-permute-start.32 = (bf16[2,128,256]{2,1,0:T(8,128)(2,1)S(1)}, bf16[2,128,256]{2,1,0:T(8,128)(2,1)S(1)}, u32[]{:S(2)}, u32[]{:S(2)}) collective-permute-start(bf16[2,128,256]{2,1,0:T(8,128)(2,1)S(1)} %get-tuple-element.98), channel_id=1, source_target_pairs={{0,32},{8,40},{16,48},{24,56},{32,0},{40,8},{48,16},{56,24},{64,96... | collective-permute-start | bytes 393224 | tf_op jit(solution)/shard_map/ppermute | solution.py:15
  82.6 2.1 %collective-permute-start.28 = (bf16[2,128,256]{2,1,0:T(8,128)(2,1)S(1)}, bf16[2,128,256]{2,1,0:T(8,128)(2,1)S(1)}, u32[]{:S(2)}, u32[]{:S(2)}) collective-permute-start(bf16[2,128,256]{2,1,0:T(8,128)(2,1)S(1)} %get-tuple-element.99), channel_id=1, source_target_pairs={{0,4},{1,5},{2,6},{3,7},{4,0},{5,1},{6,2},{7,3},{8,12},{9,13},{10,... | collective-permute-start | bytes 393224 | tf_op jit(solution)/shard_map/ppermute | solution.py:15
  86.3 2.0 %collective-permute-start.30 = (bf16[2,128,256]{2,1,0:T(8,128)(2,1)S(1)}, bf16[2,128,256]{2,1,0:T(8,128)(2,1)S(1)}, u32[]{:S(2)}, u32[]{:S(2)}) collective-permute-start(bf16[2,128,256]{2,1,0:T(8,128)(2,1)S(1)} %get-tuple-element.100), channel_id=1, source_target_pairs={{0,6},{1,7},{2,4},{3,5},{4,2},{5,3},{6,0},{7,1},{8,14},{9,15},{10,... | collective-permute-start | bytes 393224 | tf_op jit(solution)/shard_map/ppermute | solution.py:15
  88.7 1.9 %collective-permute-done.28 = bf16[2,128,256]{2,1,0:T(8,128)(2,1)S(1)} collective-permute-done((bf16[2,128,256]{2,1,0:T(8,128)(2,1)S(1)}, bf16[2,128,256]{2,1,0:T(8,128)(2,1)S(1)}, u32[]{:S(2)}, u32[]{:S(2)}) %collective-permute-start.28) | collective-permute-done | bytes 131104 | tf_op jit(solution)/shard_map/ppermute | solution.py:15
  90.6 2.3 %collective-permute-start.35 = (bf16[2,128,256]{2,1,0:T(8,128)(2,1)S(1)}, bf16[2,128,256]{2,1,0:T(8,128)(2,1)S(1)}, u32[]{:S(2)}, u32[]{:S(2)}) collective-permute-start(bf16[2,128,256]{2,1,0:T(8,128)(2,1)S(1)} %fusion.23), channel_id=1, source_target_pairs={{0,64},{8,72},{16,80},{24,88},{32,96},{40,104},{48,112},{56,120},{... | collective-permute-start | bytes 393224 | tf_op jit(solution)/shard_map/ppermute | solution.py:15
  93.6 3.6 %collective-permute-done.35 = bf16[2,128,256]{2,1,0:T(8,128)(2,1)S(1)} collective-permute-done((bf16[2,128,256]{2,1,0:T(8,128)(2,1)S(1)}, bf16[2,128,256]{2,1,0:T(8,128)(2,1)S(1)}, u32[]{:S(2)}, u32[]{:S(2)}) %collective-permute-start.35) | collective-permute-done | bytes 131104 | tf_op jit(solution)/shard_map/ppermute | solution.py:15
  97.4 3.3 %collective-permute-start.39 = (bf16[2,128,256]{2,1,0:T(8,128)(2,1)S(1)}, bf16[2,128,256]{2,1,0:T(8,128)(2,1)S(1)}, u32[]{:S(2)}, u32[]{:S(2)}) collective-permute-start(bf16[2,128,256]{2,1,0:T(8,128)(2,1)S(1)} %get-tuple-element.58), channel_id=1, source_target_pairs={{0,32},{8,40},{16,48},{24,56},{32,0},{40,8},{48,16},{56,24},{64,96... | collective-permute-start | bytes 393224 | tf_op jit(solution)/shard_map/ppermute | solution.py:15
  110.9 3.5 %collective-permute-done.36 = bf16[2,128,256]{2,1,0:T(8,128)(2,1)S(1)} collective-permute-done((bf16[2,128,256]{2,1,0:T(8,128)(2,1)S(1)}, bf16[2,128,256]{2,1,0:T(8,128)(2,1)S(1)}, u32[]{:S(2)}, u32[]{:S(2)}) %collective-permute-start.36) | collective-permute-done | bytes 131104 | tf_op jit(solution)/shard_map/ppermute | solution.py:15
  121.9 3.2 %collective-permute-start.48 = (bf16[2,128,256]{2,1,0:T(8,128)(2,1)S(1)}, bf16[2,128,256]{2,1,0:T(8,128)(2,1)S(1)}, u32[]{:S(2)}, u32[]{:S(2)}) collective-permute-start(bf16[2,128,256]{2,1,0:T(8,128)(2,1)S(1)} %get-tuple-element.82), channel_id=1, source_target_pairs={{0,32},{8,40},{16,48},{24,56},{32,0},{40,8},{48,16},{56,24},{64,96... | collective-permute-start | bytes 393224 | tf_op jit(solution)/shard_map/ppermute | solution.py:15
  132.3 2.2 %collective-permute-done.44 = bf16[2,128,256]{2,1,0:T(8,128)(2,1)S(1)} collective-permute-done((bf16[2,128,256]{2,1,0:T(8,128)(2,1)}, bf16[2,128,256]{2,1,0:T(8,128)(2,1)S(1)}, u32[]{:S(2)}, u32[]{:S(2)}) %collective-permute-start.44) | collective-permute-done | bytes 131104 | tf_op jit(solution)/shard_map/ppermute | solution.py:15
  134.6 2.5 %collective-permute-start.51 = (bf16[128,256]{1,0:T(8,128)(2,1)S(1)}, bf16[128,256]{1,0:T(8,128)(2,1)S(1)}, u32[]{:S(2)}, u32[]{:S(2)}) collective-permute-start(bf16[128,256]{1,0:T(8,128)(2,1)S(1)} %dynamic-slice_bitcast_fusion.18), channel_id=1, source_target_pairs={{0,64},{8,72},{16,80},{24,88},{32,96},{40,104},{48,112},{56,120},{... | collective-permute-start | bytes 196616 | tf_op jit(solution)/shard_map/ppermute | solution.py:15
  138.2 2.5 %collective-permute-done.51 = bf16[128,256]{1,0:T(8,128)(2,1)S(1)} collective-permute-done((bf16[128,256]{1,0:T(8,128)(2,1)S(1)}, bf16[128,256]{1,0:T(8,128)(2,1)S(1)}, u32[]{:S(2)}, u32[]{:S(2)}) %collective-permute-start.51) | collective-permute-done | bytes 65568 | tf_op jit(solution)/shard_map/ppermute | solution.py:15
  (176 shorter events, 69.8 us)
Async XLA Ops:
  1.7 11.0 %collective-permute-start.5 = (bf16[128,256]{1,0:T(8,128)(2,1)S(1)}, bf16[128,256]{1,0:T(8,128)(2,1)S(1)}, u32[]{:S(2)}, u32[]{:S(2)}) collective-permute-start(bf16[128,256]{1,0:T(8,128)(2,1)S(1)} %get-tuple-element.63), channel_id=1, source_target_pairs={{0,64},{8,72},{16,80},{24,88},{32,96},{40,104},{48,112},{56,120},{... | collective-permute-start | bytes 196616 | tf_op jit(solution)/shard_map/ppermute | solution.py:15
  6.7 10.1 %collective-permute-start = (bf16[128,256]{1,0:T(8,128)(2,1)S(1)}, bf16[128,256]{1,0:T(8,128)(2,1)S(1)}, u32[]{:S(2)}, u32[]{:S(2)}) collective-permute-start(bf16[128,256]{1,0:T(8,128)(2,1)S(1)} %get-tuple-element.65), channel_id=1, source_target_pairs={{0,1},{1,0},{2,3},{3,2},{4,5},{5,4},{6,7},{7,6},{8,9},{9,8},{10,11... | collective-permute-start | bytes 196616 | tf_op jit(solution)/shard_map/ppermute | solution.py:15
  8.8 8.5 %collective-permute-start.18 = (bf16[2,128,256]{2,1,0:T(8,128)(2,1)S(1)}, bf16[2,128,256]{2,1,0:T(8,128)(2,1)S(1)}, u32[]{:S(2)}, u32[]{:S(2)}) collective-permute-start(bf16[2,128,256]{2,1,0:T(8,128)(2,1)S(1)} %pad_maximum_fusion.18), channel_id=1, source_target_pairs={{0,64},{8,72},{16,80},{24,88},{32,96},{40,104},{48,112},{56,120},{... | collective-permute-start | bytes 393224 | tf_op jit(solution)/shard_map/ppermute | solution.py:15
  10.9 9.5 %collective-permute-start.1 = (bf16[2,128,256]{2,1,0:T(8,128)(2,1)S(1)}, bf16[2,128,256]{2,1,0:T(8,128)(2,1)S(1)}, u32[]{:S(2)}, u32[]{:S(2)}) collective-permute-start(bf16[2,128,256]{2,1,0:T(8,128)(2,1)S(1)} %pad_maximum_fusion.15), channel_id=1, source_target_pairs={{0,1},{1,0},{2,3},{3,2},{4,5},{5,4},{6,7},{7,6},{8,9},{9,8},{10,11... | collective-permute-start | bytes 393224 | tf_op jit(solution)/shard_map/ppermute | solution.py:15
  12.9 8.3 %collective-permute-start.6 = (bf16[2,128,256]{2,1,0:T(8,128)(2,1)S(1)}, bf16[2,128,256]{2,1,0:T(8,128)(2,1)S(1)}, u32[]{:S(2)}, u32[]{:S(2)}) collective-permute-start(bf16[2,128,256]{2,1,0:T(8,128)(2,1)S(1)} %get-tuple-element.141), channel_id=1, source_target_pairs={{0,32},{8,40},{16,48},{24,56},{32,0},{40,8},{48,16},{56,24},{64,96... | collective-permute-start | bytes 393224 | tf_op jit(solution)/shard_map/ppermute | solution.py:15
  16.1 7.5 %collective-permute-start.7 = (bf16[2,128,256]{2,1,0:T(8,128)(2,1)S(1)}, bf16[2,128,256]{2,1,0:T(8,128)(2,1)S(1)}, u32[]{:S(2)}, u32[]{:S(2)}) collective-permute-start(bf16[2,128,256]{2,1,0:T(8,128)(2,1)S(1)} %get-tuple-element.141), channel_id=1, source_target_pairs={{0,16},{8,24},{16,0},{24,8},{32,48},{40,56},{48,32},{56,40},{64,80... | collective-permute-start | bytes 393224 | tf_op jit(solution)/shard_map/ppermute | solution.py:15
  17.3 7.5 %collective-permute-start.3 = (bf16[2,128,256]{2,1,0:T(8,128)(2,1)S(1)}, bf16[2,128,256]{2,1,0:T(8,128)(2,1)S(1)}, u32[]{:S(2)}, u32[]{:S(2)}) collective-permute-start(bf16[2,128,256]{2,1,0:T(8,128)(2,1)S(1)} %get-tuple-element.145), channel_id=1, source_target_pairs={{0,4},{1,5},{2,6},{3,7},{4,0},{5,1},{6,2},{7,3},{8,12},{9,13},{10,... | collective-permute-start | bytes 393224 | tf_op jit(solution)/shard_map/ppermute | solution.py:15
  33.4 7.9 %collective-permute-start.19 = (bf16[2,128,256]{2,1,0:T(8,128)(2,1)S(1)}, bf16[2,128,256]{2,1,0:T(8,128)(2,1)S(1)}, u32[]{:S(2)}, u32[]{:S(2)}) collective-permute-start(bf16[2,128,256]{2,1,0:T(8,128)(2,1)S(1)} %get-tuple-element.110), channel_id=1, source_target_pairs={{0,32},{8,40},{16,48},{24,56},{32,0},{40,8},{48,16},{56,24},{64,96... | collective-permute-start | bytes 393224 | tf_op jit(solution)/shard_map/ppermute | solution.py:15
  36.5 7.2 %collective-permute-start.20 = (bf16[2,128,256]{2,1,0:T(8,128)(2,1)S(1)}, bf16[2,128,256]{2,1,0:T(8,128)(2,1)S(1)}, u32[]{:S(2)}, u32[]{:S(2)}) collective-permute-start(bf16[2,128,256]{2,1,0:T(8,128)(2,1)S(1)} %get-tuple-element.109), channel_id=1, source_target_pairs={{0,16},{8,24},{16,0},{24,8},{32,48},{40,56},{48,32},{56,40},{64,80... | collective-permute-start | bytes 393224 | tf_op jit(solution)/shard_map/ppermute | solution.py:15
  37.6 8.1 %collective-permute-start.11 = (bf16[2,128,256]{2,1,0:T(8,128)(2,1)S(1)}, bf16[2,128,256]{2,1,0:T(8,128)(2,1)S(1)}, u32[]{:S(2)}, u32[]{:S(2)}) collective-permute-start(bf16[2,128,256]{2,1,0:T(8,128)(2,1)S(1)} %get-tuple-element.115), channel_id=1, source_target_pairs={{0,4},{1,5},{2,6},{3,7},{4,0},{5,1},{6,2},{7,3},{8,12},{9,13},{10,... | collective-permute-start | bytes 393224 | tf_op jit(solution)/shard_map/ppermute | solution.py:15
  39.6 10.1 %collective-permute-start.12 = (bf16[2,128,256]{2,1,0:T(8,128)(2,1)S(1)}, bf16[2,128,256]{2,1,0:T(8,128)(2,1)S(1)}, u32[]{:S(2)}, u32[]{:S(2)}) collective-permute-start(bf16[2,128,256]{2,1,0:T(8,128)(2,1)S(1)} %get-tuple-element.117), channel_id=1, source_target_pairs={{0,2},{1,3},{2,0},{3,1},{4,6},{5,7},{6,4},{7,5},{8,10},{9,11},{10,... | collective-permute-start | bytes 393224 | tf_op jit(solution)/shard_map/ppermute | solution.py:15
  41.4 8.4 %collective-permute-start.13 = (bf16[2,128,256]{2,1,0:T(8,128)(2,1)S(1)}, bf16[2,128,256]{2,1,0:T(8,128)(2,1)S(1)}, u32[]{:S(2)}, u32[]{:S(2)}) collective-permute-start(bf16[2,128,256]{2,1,0:T(8,128)(2,1)S(1)} %get-tuple-element.116), channel_id=1, source_target_pairs={{0,6},{1,7},{2,4},{3,5},{4,2},{5,3},{6,0},{7,1},{8,14},{9,15},{10,... | collective-permute-start | bytes 393224 | tf_op jit(solution)/shard_map/ppermute | solution.py:15
  45.8 7.9 %collective-permute-start.22 = (bf16[2,128,256]{2,1,0:T(8,128)(2,1)S(1)}, bf16[2,128,256]{2,1,0:T(8,128)(2,1)S(1)}, u32[]{:S(2)}, u32[]{:S(2)}) collective-permute-start(bf16[2,128,256]{2,1,0:T(8,128)(2,1)S(1)} %fusion.29), channel_id=1, source_target_pairs={{0,64},{8,72},{16,80},{24,88},{32,96},{40,104},{48,112},{56,120},{... | collective-permute-start | bytes 393224 | tf_op jit(solution)/shard_map/ppermute | solution.py:15
  49.8 8.3 %collective-permute-start.14 = (bf16[2,128,256]{2,1,0:T(8,128)(2,1)S(1)}, bf16[2,128,256]{2,1,0:T(8,128)(2,1)S(1)}, u32[]{:S(2)}, u32[]{:S(2)}) collective-permute-start(bf16[2,128,256]{2,1,0:T(8,128)(2,1)S(1)} %fusion.32), channel_id=1, source_target_pairs={{0,1},{1,0},{2,3},{3,2},{4,5},{5,4},{6,7},{7,6},{8,9},{9,8},{10,11... | collective-permute-start | bytes 393224 | tf_op jit(solution)/shard_map/ppermute | solution.py:15
  65.0 7.5 %collective-permute-start.26 = (bf16[4,2,128,256]{3,2,1,0:T(8,128)(2,1)S(1)}, bf16[4,2,128,256]{3,2,1,0:T(8,128)(2,1)S(1)}, u32[]{:S(2)}, u32[]{:S(2)}) collective-permute-start(bf16[4,2,128,256]{3,2,1,0:T(8,128)(2,1)S(1)} %get-tuple-element.102), channel_id=1, source_target_pairs={{0,8},{8,0},{16,24},{24,16},{32,40},{40,32},{48,56},{56,48},{64,72... | collective-permute-start | bytes 1572872 | tf_op jit(solution)/shard_map/ppermute | solution.py:15
  78.3 7.9 %collective-permute-start.32 = (bf16[2,128,256]{2,1,0:T(8,128)(2,1)S(1)}, bf16[2,128,256]{2,1,0:T(8,128)(2,1)S(1)}, u32[]{:S(2)}, u32[]{:S(2)}) collective-permute-start(bf16[2,128,256]{2,1,0:T(8,128)(2,1)S(1)} %get-tuple-element.98), channel_id=1, source_target_pairs={{0,32},{8,40},{16,48},{24,56},{32,0},{40,8},{48,16},{56,24},{64,96... | collective-permute-start | bytes 393224 | tf_op jit(solution)/shard_map/ppermute | solution.py:15
  82.6 8.0 %collective-permute-start.28 = (bf16[2,128,256]{2,1,0:T(8,128)(2,1)S(1)}, bf16[2,128,256]{2,1,0:T(8,128)(2,1)S(1)}, u32[]{:S(2)}, u32[]{:S(2)}) collective-permute-start(bf16[2,128,256]{2,1,0:T(8,128)(2,1)S(1)} %get-tuple-element.99), channel_id=1, source_target_pairs={{0,4},{1,5},{2,6},{3,7},{4,0},{5,1},{6,2},{7,3},{8,12},{9,13},{10,... | collective-permute-start | bytes 393224 | tf_op jit(solution)/shard_map/ppermute | solution.py:15
  84.7 8.3 %collective-permute-start.29 = (bf16[2,128,256]{2,1,0:T(8,128)(2,1)S(1)}, bf16[2,128,256]{2,1,0:T(8,128)(2,1)S(1)}, u32[]{:S(2)}, u32[]{:S(2)}) collective-permute-start(bf16[2,128,256]{2,1,0:T(8,128)(2,1)S(1)} %get-tuple-element.101), channel_id=1, source_target_pairs={{0,2},{1,3},{2,0},{3,1},{4,6},{5,7},{6,4},{7,5},{8,10},{9,11},{10,... | collective-permute-start | bytes 393224 | tf_op jit(solution)/shard_map/ppermute | solution.py:15
  93.0 8.5 %collective-permute-start.31 = (bf16[2,128,256]{2,1,0:T(8,128)(2,1)S(1)}, bf16[2,128,256]{2,1,0:T(8,128)(2,1)S(1)}, u32[]{:S(2)}, u32[]{:S(2)}) collective-permute-start(bf16[2,128,256]{2,1,0:T(8,128)(2,1)S(1)} %fusion.26), channel_id=1, source_target_pairs={{0,1},{1,0},{2,3},{3,2},{4,5},{5,4},{6,7},{7,6},{8,9},{9,8},{10,11... | collective-permute-start | bytes 393224 | tf_op jit(solution)/shard_map/ppermute | solution.py:15
  108.5 7.6 %collective-permute-start.42 = (bf16[4,2,128,256]{3,2,1,0:T(8,128)(2,1)S(1)}, bf16[4,2,128,256]{3,2,1,0:T(8,128)(2,1)S(1)}, u32[]{:S(2)}, u32[]{:S(2)}) collective-permute-start(bf16[4,2,128,256]{3,2,1,0:T(8,128)(2,1)S(1)} %get-tuple-element.86), channel_id=1, source_target_pairs={{0,8},{8,0},{16,24},{24,16},{32,40},{40,32},{48,56},{56,48},{64,72... | collective-permute-start | bytes 1572872 | tf_op jit(solution)/shard_map/ppermute | solution.py:15
  121.9 9.0 %collective-permute-start.48 = (bf16[2,128,256]{2,1,0:T(8,128)(2,1)S(1)}, bf16[2,128,256]{2,1,0:T(8,128)(2,1)S(1)}, u32[]{:S(2)}, u32[]{:S(2)}) collective-permute-start(bf16[2,128,256]{2,1,0:T(8,128)(2,1)S(1)} %get-tuple-element.82), channel_id=1, source_target_pairs={{0,32},{8,40},{16,48},{24,56},{32,0},{40,8},{48,16},{56,24},{64,96... | collective-permute-start | bytes 393224 | tf_op jit(solution)/shard_map/ppermute | solution.py:15
  125.1 7.2 %collective-permute-start.49 = (bf16[2,128,256]{2,1,0:T(8,128)(2,1)S(1)}, bf16[2,128,256]{2,1,0:T(8,128)(2,1)S(1)}, u32[]{:S(2)}, u32[]{:S(2)}) collective-permute-start(bf16[2,128,256]{2,1,0:T(8,128)(2,1)S(1)} %get-tuple-element.81), channel_id=1, source_target_pairs={{0,16},{8,24},{16,0},{24,8},{32,48},{40,56},{48,32},{56,40},{64,80... | collective-permute-start | bytes 393224 | tf_op jit(solution)/shard_map/ppermute | solution.py:15
  126.8 7.8 %collective-permute-start.44 = (bf16[2,128,256]{2,1,0:T(8,128)(2,1)}, bf16[2,128,256]{2,1,0:T(8,128)(2,1)S(1)}, u32[]{:S(2)}, u32[]{:S(2)}) collective-permute-start(bf16[2,128,256]{2,1,0:T(8,128)(2,1)} %get-tuple-element.83), channel_id=1, source_target_pairs={{0,4},{1,5},{2,6},{3,7},{4,0},{5,1},{6,2},{7,3},{8,12},{9,13},{10,... | collective-permute-start | bytes 393224 | tf_op jit(solution)/shard_map/ppermute | solution.py:15
  129.7 7.4 %collective-permute-start.45 = (bf16[2,128,256]{2,1,0:T(8,128)(2,1)S(1)}, bf16[2,128,256]{2,1,0:T(8,128)(2,1)S(1)}, u32[]{:S(2)}, u32[]{:S(2)}) collective-permute-start(bf16[2,128,256]{2,1,0:T(8,128)(2,1)S(1)} %get-tuple-element.85), channel_id=1, source_target_pairs={{0,2},{1,3},{2,0},{3,1},{4,6},{5,7},{6,4},{7,5},{8,10},{9,11},{10,... | collective-permute-start | bytes 393224 | tf_op jit(solution)/shard_map/ppermute | solution.py:15
  (33 other events, 203.0 us)
